TPU v7x, 256 devices: a whole 4x4x8 slice. The times are simulated.
256 devices in a mesh: batch: 8 (over z), col: 32 (over y, x, core).
Axes of the slice: x: 4, y: 4, z: 8, core: 2. Of those that a mesh axis runs over, the one named last changes fastest.
Arguments:
- views: bfloat16 [2, 1024, 4096], P(None, 'batch', 'col'), may hold values from -132 to 132
- norm_scale_gain: float32 [4096], P('col'), may hold values from 0.5 to 1.5
- norm_shift_bias: float32 [4096], P('col'), may hold values from -3 to 3
- weight: bfloat16 [4096, 8192], P(None, 'col'), may hold values from -0.09375 to 0.09375
Outputs:
- loss: float32 [], replicated
- grad_weight: float32 [4096, 8192], P('batch', 'col')
- grad_gain: float32 [4096], P('col')
- grad_bias: float32 [4096], P('col')
- views_gradient: float32 [2, 1024, 4096], P(None, 'batch', 'col')
All inputs are finite; a program needn't handle non-finite values.
Results may differ from a plain program's by a relative error of at most 0.0027.
Values may be sent and summed in bfloat16 or wider, within the bound.
A program may use at most 64 MiB of HBM per device.

v0:
```python
import jax
import jax.numpy as jnp
from jax import lax
from jax.sharding import PartitionSpec as P

E = 8192


eps_norm = 1e-05
eps_std = 0.0001


def gelu_slope(preactivation):
    value, pullback = jax.vjp(lambda t: jax.nn.gelu(t, approximate=True), preactivation)
    return pullback(jnp.ones_like(value))[0]


def shards(views, norm_scale_gain, norm_shift_bias, weight):
    n_batch = lax.axis_size("batch")
    n_col = lax.axis_size("col")
    local_rows = views.shape[1]
    sample_count = local_rows * n_batch
    scale = sample_count * E / 128.0
    hidden_float = views.astype(jnp.float32)
    total = lax.psum(jnp.sum(hidden_float, axis=1), "batch")
    batch_average = total[:, None, :] / sample_count
    centred = hidden_float - batch_average
    spread = lax.psum(jnp.sum(centred * centred, axis=1), "batch")
    var = spread[:, None, :] / sample_count
    inverse_deviation = 1.0 / jnp.sqrt(var + eps_norm)
    normalised_input = (hidden_float - batch_average) * inverse_deviation
    preactivation = norm_scale_gain * normalised_input + norm_shift_bias
    act = jax.nn.gelu(preactivation, approximate=True).astype(jnp.bfloat16)
    act_full = lax.all_gather(act, "col", axis=2, tiled=True)
    z_local = jnp.einsum(
        "vrk,kj->vrj", act_full, weight, preferred_element_type=jnp.float32
    ).astype(jnp.bfloat16)
    z_all = lax.all_gather(z_local, "batch", axis=1, tiled=True)
    zf_all = z_all.astype(jnp.float32)
    zmean = jnp.mean(zf_all, axis=1, keepdims=True)
    zc_all = zf_all - zmean
    zvar = jnp.sum(zc_all * zc_all, axis=1, keepdims=True) / (sample_count - 1)
    std = jnp.sqrt(zvar + eps_std)
    zcb_all = zc_all.astype(jnp.bfloat16)
    offset = lax.axis_index("batch") * local_rows
    zc_loc = lax.dynamic_slice_in_dim(zc_all, offset, local_rows, 1)
    zcb_loc = zc_loc.astype(jnp.bfloat16)
    diag = jnp.sum(jnp.square(zcb_all.astype(jnp.float32)), axis=1, keepdims=True)
    kernel_part = jnp.einsum("vrj,vmj->vrm", zcb_loc, zcb_all, preferred_element_type=jnp.float32)
    kernel = lax.psum(kernel_part, "col")
    kernel_b = kernel.astype(jnp.bfloat16)
    denom = float((sample_count - 1) ** 2 * E)
    coef = 4.0 * scale / denom
    hinge_coef = 25.0 * scale / (2.0 * E * (sample_count - 1))
    mask = jnp.where(std < 1.0, 1.0, 0.0)
    moved = jnp.einsum("vrm,vmj->vrj", kernel_b, zcb_all, preferred_element_type=jnp.float32)
    g_cov = coef * (moved - zcb_loc.astype(jnp.float32) * diag)
    g_var = -hinge_coef * mask * zc_loc / std
    summed = g_cov + g_var
    col_total = lax.psum(jnp.sum(summed, axis=1), "batch")
    zf_loc = z_local.astype(jnp.float32)
    diff = zf_loc[0] - zf_loc[1]
    g_inv = 50.0 * scale / (sample_count * E) * diff
    dz = summed - col_total[:, None, :] / sample_count + jnp.stack([g_inv, -g_inv])
    dzb = dz.astype(jnp.bfloat16)
    inv_share = jnp.sum(diff * diff) / (sample_count * E)
    hinge_share = jnp.sum(jnp.maximum(1.0 - std, 0.0)) / (2 * E)
    block_share = jnp.sum(kernel * kernel) / denom
    diag_share = jnp.sum(diag * diag) / denom
    share = 25.0 * inv_share + (25.0 * hinge_share - diag_share) / n_batch + block_share / n_col
    loss = lax.psum(share, ("batch", "col"))
    d_act_t = lax.psum_scatter(
        jnp.einsum("kj,vrj->kvr", weight, dzb, preferred_element_type=jnp.float32),
        "col",
        scatter_dimension=0,
        tiled=True,
    )
    d_act = jnp.transpose(d_act_t, (1, 2, 0))
    grad_weight = lax.psum_scatter(
        jnp.einsum("vrk,vrj->kj", act_full, dzb, preferred_element_type=jnp.float32),
        "batch",
        scatter_dimension=0,
        tiled=True,
    )
    preactivation_gradient = d_act * gelu_slope(preactivation)
    bias_gradient_sum, gain_gradient_sum = lax.psum(
        (
            jnp.sum(preactivation_gradient, axis=1),
            jnp.sum(preactivation_gradient * normalised_input, axis=1),
        ),
        "batch",
    )
    grad_bias = jnp.sum(bias_gradient_sum, axis=0)
    grad_gain = jnp.sum(gain_gradient_sum, axis=0)
    views_gradient = (
        norm_scale_gain
        * (
            preactivation_gradient
            - bias_gradient_sum[:, None, :] / sample_count
            - normalised_input * gain_gradient_sum[:, None, :] / sample_count
        )
        * inverse_deviation
    )
    return (loss, grad_weight, grad_gain, grad_bias, views_gradient)


def solution(mesh):
    placed = (P(None, "batch", "col"), P("col"), P("col"), P(None, "col"))
    return jax.shard_map(
        shards,
        mesh=mesh,
        in_specs=placed,
        out_specs=(P(), P("batch", "col"), P("col"), P("col"), P(None, "batch", "col")),
        check_vma=False,
    )
```

profile of v0, /device:TPU:8, one launch (start us, length us, event | category | flops | bytes accessed | tf_op | source)
XLA Modules:
  0.0 429.3 jit_solution(8545685748164966906)
XLA Ops:
  7.2 0.0 copy-start
  7.2 0.0 all-gather.3.cloned.1.call-start
  7.2 1.0 convert_reduce_fusion.1
  8.2 20.0 %psum.49 = f32[2,128]{1,0:T(2,128)S(1)} all-reduce(f32[2,128]{1,0:T(2,128)S(1)} %convert_reduce_fusion.1), channel_id=1, replica_groups=mesh['batch'=8,'col'=32] {'batch'}, use_global_device_ids=true, to_apply=%region_1.0 | all-reduce | flops 256 | bytes 2048 | tf_op jit(solution)/shard_map/psum | solution.py:25
  28.3 0.9 fusion.32
  29.1 14.2 %psum.50 = f32[2,128]{1,0:T(2,128)S(1)} all-reduce(f32[2,128]{1,0:T(2,128)S(1)} %fusion.32), channel_id=1, replica_groups=mesh['batch'=8,'col'=32] {'batch'}, use_global_device_ids=true, to_apply=%region_3.0 | all-reduce | flops 256 | bytes 2048 | tf_op jit(solution)/shard_map/psum | solution.py:28
  43.3 1.6 fusion.25
  44.9 0.0 all-gather.3.cloned.1.call-update
  44.9 0.0 all-gather.5.cloned.1.call-start
  44.9 48.6 %all-gather.3.cloned.1.call-done = bf16[2,128,4096]{2,1,0:T(8,128)(2,1)} async-done(((bf16[2,128,128]{2,1,0:T(8,128)(2,1)}), bf16[2,128,4096]{2,1,0:T(8,128)(2,1)}) %all-gather.3.cloned.1.call-update) | async-done | bytes 2097168 | tf_op jit(solution)/shard_map/all_gather | solution.py:34
  93.5 0.0 copy-done
  93.5 3.0 fusion.42
  96.5 0.0 all-gather.5.cloned.1.call-update
  96.5 0.0 all-reduce.3.cloned.1.call-start
  96.5 38.7 %all-gather.5.cloned.1.call-done = bf16[2,1024,256]{2,1,0:T(8,128)(2,1)} async-done(((bf16[2,128,256]{2,1,0:T(8,128)(2,1)}), bf16[2,1024,256]{2,1,0:T(8,128)(2,1)}) %all-gather.5.cloned.1.call-update) | async-done | bytes 1048592 | tf_op jit(solution)/shard_map/all_gather | solution.py:38
  135.2 0.0 copy-start.1
  135.2 1.5 convert_reduce_fusion
  136.7 2.1 multiply_reduce_fusion
  138.8 0.0 copy-start.2
  138.8 1.3 copy-done.2
  140.2 0.0 copy-done.1
  140.2 1.5 fusion.10
  141.7 0.0 all-reduce.3.cloned.1.call-update
  141.7 0.0 reduce-scatter.5.cloned.1.call-start
  141.7 1.3 fusion.41
  143.0 0.0 copy-start.5
  143.0 1.3 fusion.37
  144.4 110.0 %all-reduce.3.cloned.1.call-done = f32[2,128,1024]{2,1,0:T(8,128)} async-done(((f32[2,128,1024]{2,1,0:T(8,128)}), f32[2,128,1024]{2,1,0:T(8,128)}) %all-reduce.3.cloned.1.call-update) | async-done | bytes 1048592 | tf_op jit(solution)/shard_map/psum | solution.py:50
  254.4 2.3 fusion.43
  256.7 17.4 %psum.53 = f32[2,256]{1,0:T(2,128)S(1)} all-reduce(f32[2,256]{1,0:T(2,128)S(1)} %get-tuple-element.23), channel_id=1, replica_groups=mesh['batch'=8,'col'=32] {'batch'}, use_global_device_ids=true, to_apply=%region_14.15 | all-reduce | flops 512 | bytes 4096 | tf_op jit(solution)/shard_map/psum | solution.py:60
  274.2 0.0 copy-done.5
  274.2 1.0 fusion.13
  275.2 2.7 convolution_bitcast_fusion
  277.9 0.0 reduce-scatter.5.cloned.1.call-update
  277.9 0.0 reduce-scatter.3.cloned.1.call-start
  278.0 4.3 convolution_bitcast_fusion.1
  282.2 0.0 copy-start.4
  282.3 0.0 copy-start.3
  282.3 0.0 copy-start.6
  282.3 0.0 copy-start.7
  282.3 0.0 reduce-scatter.3.cloned.1.call-update
  283.7 0.6 multiply_reduce_fusion.4
  284.9 0.0 copy-done.4
  284.9 0.9 multiply_reduce_fusion.2
  286.5 72.5 %psum.52 = f32[]{:T(128)} all-reduce(f32[]{:T(128)S(6)} %add.83), channel_id=1, replica_groups=mesh['batch'=8,'col'=32] {'batch','col'}, use_global_device_ids=true, to_apply=%region_12.13 | all-reduce | flops 1 | bytes 8 | tf_op jit(solution)/shard_map/psum | solution.py:71
  359.0 5.7 %reduce-scatter.5.cloned.1.call-done = f32[128,2,128]{0,2,1:T(8,128)} async-done(((f32[4096,2,128]{0,2,1:T(8,128)}), f32[128,2,128]{0,2,1:T(8,128)}) %reduce-scatter.5.cloned.1.call-update) | async-done | bytes 131088 | tf_op jit(solution)/shard_map/reduce_scatter | solution.py:72
  364.7 0.0 copy-done.3
  364.7 0.0 copy-done.6
  364.7 0.0 copy-done.7
  364.7 1.0 fusion.39
  365.7 17.4 %all-reduce = (f32[2,128]{1,0:T(2,128)S(1)}, f32[2,128]{1,0:T(2,128)S(1)}) all-reduce(f32[2,128]{1,0:T(2,128)S(1)} %get-tuple-element.8, f32[2,128]{1,0:T(2,128)S(1)} %get-tuple-element.7), channel_id=1, replica_groups=mesh['batch'=8,'col'=32] {'batch'}, use_global_device_ids=true, to_apply=%region_18.19 | all-reduce | flops 512 | bytes 4096 | tf_op jit(solution)/shard_map/psum | solution.py:86
  383.1 0.5 reduce_sum.137
  383.7 0.5 broadcast_multiply_fusion.3
  384.2 0.7 fusion.31
  384.9 37.9 %reduce-scatter.3.cloned.1.call-done = f32[512,256]{1,0:T(8,128)} async-done(((f32[4096,256]{1,0:T(8,128)}), f32[512,256]{1,0:T(8,128)}) %reduce-scatter.3.cloned.1.call-update) | async-done | bytes 524304 | tf_op jit(solution)/shard_map/reduce_scatter | solution.py:79
  (4 shorter events, 0.0 us)
Async XLA Ops:
  7.2 86.3 %copy-start = (bf16[4096,256]{1,0:T(8,128)(2,1)S(1)}, bf16[4096,256]{1,0:T(8,128)(2,1)}, u32[]{:S(2)}) copy-start(bf16[4096,256]{1,0:T(8,128)(2,1)} %param.7) | copy-start | bytes 6291460
  7.2 86.3 %all-gather.3.cloned.1.call-start = ((), (), s32[]{:S(2)}) async-start(), calls=%async_computation.2 | async-start | bytes 2162688 | tf_op jit(solution)/shard_map/all_gather | solution.py:34
  44.9 90.3 %all-gather.5.cloned.1.call-start = ((), (), s32[]{:S(2)}) async-start(), calls=%async_computation.3 | async-start | bytes 1179648 | tf_op jit(solution)/shard_map/all_gather | solution.py:38
  96.5 157.9 %all-reduce.3.cloned.1.call-start = ((), (), s32[]{:S(2)}) async-start(), calls=%async_computation.4 | async-start | bytes 2097152 | tf_op jit(solution)/shard_map/psum | solution.py:50
  135.2 5.0 %copy-start.1 = (bf16[2,1024,256]{2,1,0:T(8,128)(2,1)S(1)}, bf16[2,1024,256]{2,1,0:T(8,128)(2,1)}, u32[]{:S(2)}) copy-start(bf16[2,1024,256]{2,1,0:T(8,128)(2,1)} %all-gather.5.cloned.1.call-done) | copy-start | bytes 3145732
  138.8 1.4 copy-start.2
  141.7 223.0 %reduce-scatter.5.cloned.1.call-start = ((), (), s32[]{:S(2)}) async-start(), calls=%async_computation.6 | async-start | bytes 4325376 | tf_op jit(solution)/shard_map/reduce_scatter | solution.py:72
  143.0 131.2 %copy-start.5 = (f32[1,128,256]{2,1,0:T(8,128)S(1)}, f32[1,128,256]{2,1,0:T(8,128)}, u32[]{:S(2)}) copy-start(f32[1,128,256]{2,1,0:T(8,128)} %get-tuple-element.13) | copy-start | bytes 393220
  277.9 144.9 %reduce-scatter.3.cloned.1.call-start = ((), (), s32[]{:S(2)}) async-start(), calls=%async_computation.5 | async-start | bytes 4718592 | tf_op jit(solution)/shard_map/reduce_scatter | solution.py:79
  282.2 2.7 copy-start.4
  282.3 82.4 %copy-start.3 = (bf16[2,128,128]{2,1,0:T(8,128)(2,1)S(1)}, bf16[2,128,128]{2,1,0:T(8,128)(2,1)}, u32[]{:S(2)}) copy-start(bf16[2,128,128]{2,1,0:T(8,128)(2,1)} %param.4) | copy-start | bytes 196612
  282.3 82.4 %copy-start.6 = (f32[128]{0:T(128)S(1)}, f32[128]{0:T(128)}, u32[]{:S(2)}) copy-start(f32[128]{0:T(128)} %param.5) | copy-start | bytes 1540
  282.3 82.4 %copy-start.7 = (f32[128]{0:T(128)S(1)}, f32[128]{0:T(128)}, u32[]{:S(2)}) copy-start(f32[128]{0:T(128)} %param.6) | copy-start | bytes 1540
Sparse Core Ops, SparseCore 0:
  45.0 48.4 all-gather.2
  96.6 38.5 all-gather.4
  141.8 112.5 all-reduce.2
  278.0 86.6 reduce-scatter.4
  367.7 55.0 reduce-scatter.2
where the time goes:
time: 431 us; the launch traced here: 429 us
  waiting for transfers between devices  241 us (56%)
  blocking collectives  142 us (33%)
  between operations  16.5 us (4%)
  other arithmetic  14.9 us (3%)
  matrix products  13.8 us (3%)
    psum x1, waiting for transfers between devices, shards(): kernel = lax.psum(kernel_part, 'col')  110 us
    psum x1, blocking collectives, shards(): loss = lax.psum(share, ('batch', 'col'))  72.5 us
    all_gather x1, waiting for transfers between devices, shards(): act_full = lax.all_gather(act, 'col', axis=2, tiled=True)  48.6 us
    all_gather x1, waiting for transfers between devices, shards(): z_all = lax.all_gather(z_local, 'batch', axis=1, tiled=True)  38.7 us
    reduce_scatter x1, waiting for transfers between devices, shards(): lax.psum_scatter(jnp.einsum('vrk,vrj->kj', act_full, dzb, preferred_eleme...  37.9 us
    psum x1, blocking collectives, shards(): total = lax.psum(jnp.sum(hidden_float, axis=1), 'batch')  20 us
    psum x1, blocking collectives, shards(): col_total = lax.psum(jnp.sum(summed, axis=1), 'batch')  17.4 us
    psum x1, blocking collectives, shards(): lax.psum((jnp.sum(preactivation_gradient, axis=1), jnp.sum(preactivation_...  17.4 us
  transfers between devices with their start and end apart: 5, of which 5 were waited for; matrix products, arithmetic and copies ran while one was open for 3% of the time, Pallas kernels for 0%

commit v1 on v0

v1 whole, which is shorter than its diff:
```python
import jax
import jax.numpy as jnp
from jax import lax
from jax.experimental import pallas as pl
from jax.experimental.pallas import tpu as pltpu
from jax.sharding import PartitionSpec as P

E = 8192
ROWS = 1024
PLANES = 8
SIDE = 4

eps_norm = 1e-05
eps_std = 0.0001
scale = ROWS * E / 128.0
denom = float((ROWS - 1) ** 2 * E)
coef = 4.0 * scale / denom
hinge_coef = 25.0 * scale / (2.0 * E * (ROWS - 1))
inv_coef = 50.0 * scale / (ROWS * E)

F32 = jnp.float32
BF16 = jnp.bfloat16
MESH = pl.DeviceIdType.MESH


def dot_nt(a, b):
    return lax.dot_general(a, b, (((1,), (1,)), ((), ())), preferred_element_type=F32)


def dot_tn(a, b):
    return lax.dot_general(a, b, (((0,), (0,)), ((), ())), preferred_element_type=F32)


def dot_nn(a, b):
    return jnp.dot(a, b, preferred_element_type=F32)


class Net:
    def __init__(self, send, recv):
        self.send, self.recv, self.sent = send, recv, []
        self.z = lax.axis_index("batch")
        self.c = lax.axis_index("col")
        self.core = lax.rem(self.c, 2)
        self.chip = lax.div(self.c, 2)
        self.x = lax.rem(self.chip, SIDE)
        self.y = lax.div(self.chip, SIDE)

    def at_z(self, d):
        return (lax.rem(self.z + d, PLANES), self.c)

    def at(self, y, x):
        return (self.z, (y * SIDE + x) * 2 + self.core)

    def along(self, h, f, t):
        return self.at(t, f) if h == 0 else self.at(f, t)

    def partner(self):
        return (self.z, self.chip * 2 + 1 - self.core)

    def push(self, src, dst, device):
        i = len(self.sent)
        copy = pltpu.make_async_remote_copy(
            src_ref=src,
            dst_ref=dst,
            send_sem=self.send.at[i],
            recv_sem=self.recv.at[i],
            device_id=device,
            device_id_type=MESH,
        )
        copy.start()
        self.sent.append(copy)
        return copy

    def peers(self):
        found = [self.partner()]
        found += [self.at_z(d) for d in range(1, PLANES)]
        found += [self.at(self.y, lax.rem(self.x + d, SIDE)) for d in range(1, SIDE)]
        found += [self.at(lax.rem(self.y + d, SIDE), self.x) for d in range(1, SIDE)]
        return found


def mod4(a):
    return lax.rem(a, SIDE)


def mod8(a):
    return lax.rem(a, PLANES)


def share_z(net, buf):
    sent = [net.push(buf.at[net.z], buf.at[net.z], net.at_z(d)) for d in range(1, PLANES)]
    yield
    for copy in sent:
        copy.wait_recv()
    yield


def ring_z(net, buf):
    up, down = {}, {}
    for v in range(2):
        up[1, v] = net.push(buf.at[net.z, v], buf.at[net.z, v], net.at_z(1))
        down[1, v] = net.push(buf.at[net.z, v], buf.at[net.z, v], net.at_z(7))
    yield
    for d in range(1, 5):
        for v in range(2):
            if d < 4 or v == 0:
                up[d, v].wait_recv()
                if d < 3 or (d == 3 and v == 0):
                    block = buf.at[mod8(net.z + 8 - d), v]
                    up[d + 1, v] = net.push(block, block, net.at_z(1))
            if d < 4 or v == 1:
                down[d, v].wait_recv()
                if d < 3 or (d == 3 and v == 1):
                    block = buf.at[mod8(net.z + d), v]
                    down[d + 1, v] = net.push(block, block, net.at_z(7))
        yield


def gather_plane(net, buf, forward):
    first_at, then_at = (net.x, net.y), (net.y, net.x)

    def piece(h, f, t, s=None):
        y, x = (t, f) if h == 0 else (f, t)
        return buf.at[y, x, net.core, h] if s is None else buf.at[y, x, net.core, h, s]

    def line(h, f):
        return buf.at[:, f, net.core, 0] if h == 0 else buf.at[f, :, net.core, 1]

    def send(h, f, t, s, df, dt):
        block = piece(h, f, t, s)
        return net.push(block, block, net.along(h, mod4(first_at[h] + df), mod4(then_at[h] + dt)))

    reach = (1, 3) if forward else (1, 3, 2)
    shift = (0, 3, 1, 2)
    first, cross, tie1, tie2, over = {}, {}, {}, {}, []

    def spread(h, j):
        f = mod4(first_at[h] + shift[j])
        for d in reach:
            cross[h, j, d] = send(h, f, then_at[h], None, 0, d)

    def finish(h, j):
        f = mod4(first_at[h] + shift[j])
        for d in reach:
            cross[h, j, d].wait_recv()
            if forward:
                s = 0 if d == 1 else 1
                tie2[h, j, s] = send(h, f, mod4(then_at[h] + 4 - d), s, 0, d)

    def hand_over(h, j):
        if forward:
            for s in range(2):
                tie2[h, j, s].wait_recv()
        f = mod4(first_at[h] + shift[j])
        over.append(net.push(line(h, f), line(h, f), net.partner()))

    for h in range(2):
        for d in reach:
            first[h, d] = send(h, first_at[h], then_at[h], None, d, 0)
    for h in range(2):
        spread(h, 0)
    yield
    for h in range(2):
        first[h, 1].wait_recv()
        if forward:
            tie1[h, 0] = send(h, mod4(first_at[h] + 3), then_at[h], 0, 1, 0)
        spread(h, 1)
        first[h, 3].wait_recv()
        if forward:
            tie1[h, 1] = send(h, mod4(first_at[h] + 1), then_at[h], 1, 3, 0)
        spread(h, 2)
    for h in range(2):
        finish(h, 0)
    yield
    for h in range(2):
        if forward:
            tie1[h, 0].wait_recv()
            tie1[h, 1].wait_recv()
        else:
            first[h, 2].wait_recv()
        spread(h, 3)
    for h in range(2):
        finish(h, 1)
        finish(h, 2)
        hand_over(h, 0)
    yield
    for h in range(2):
        finish(h, 3)
        hand_over(h, 1)
        hand_over(h, 2)
    for h in range(2):
        hand_over(h, 3)
    yield
    for copy in over:
        copy.wait_recv()
    yield


def reduce_plane(net, part_ref, tie1, full1, mid, tie2, full2, out):
    first_at, then_at = (net.x, net.y), (net.y, net.x)

    def part(h, f, lo, n=2):
        return part_ref.at[0, :, lo : lo + n, f] if h == 0 else part_ref.at[1, :, f, lo : lo + n]

    def first_dev(h, d):
        return net.along(h, mod4(first_at[h] + d), then_at[h])

    def then_dev(h, d):
        return net.along(h, first_at[h], mod4(then_at[h] + d))

    a, b = {}, {}
    for h in range(2):
        f = first_at[h]
        a[h, 0] = net.push(part(h, mod4(f + 2), 0), tie1.at[h, 0], first_dev(h, 1))
        a[h, 1] = net.push(part(h, mod4(f + 2), 2), tie1.at[h, 1], first_dev(h, 3))
    for h in range(2):
        f = first_at[h]
        a[h, 2] = net.push(part(h, mod4(f + 1), 2), full1.at[h, 0, :, 2:4], first_dev(h, 1))
        a[h, 3] = net.push(part(h, mod4(f + 3), 0), full1.at[h, 1, :, 0:2], first_dev(h, 3))
    yield
    for h in range(2):
        f = first_at[h]
        for k, lo in ((0, 0), (1, 2)):
            d = 1 if k == 0 else 3
            a[h, k].wait_recv()
            mine = part(h, mod4(f + d), lo)
            mine[...] = (mine[...].astype(F32) + tie1[h, k].astype(F32)).astype(mine.dtype)
            a[h, 4 + k] = net.push(mine, full1.at[h, k, :, lo : lo + 2], first_dev(h, d))
    yield
    for h in range(2):
        f, t = first_at[h], then_at[h]
        for k in range(2, 6):
            a[h, k].wait_recv()
        mine = part(h, f, 0, 4)
        mid[h] = mine[...].astype(F32) + full1[h, 0].astype(F32) + full1[h, 1].astype(F32)
        b[h, 0] = net.push(mid.at[h, 0, mod4(t + 2)], tie2.at[h, 0], then_dev(h, 1))
        b[h, 1] = net.push(mid.at[h, 1, mod4(t + 2)], tie2.at[h, 1], then_dev(h, 3))
        b[h, 2] = net.push(mid.at[h, 1, mod4(t + 1)], full2.at[h, 0, 1], then_dev(h, 1))
        b[h, 3] = net.push(mid.at[h, 0, mod4(t + 3)], full2.at[h, 1, 0], then_dev(h, 3))
    yield
    for h in range(2):
        t = then_at[h]
        for k in range(2):
            d = 1 if k == 0 else 3
            b[h, k].wait_recv()
            mine = mid.at[h, k, mod4(t + d)]
            mine[...] = mine[...] + tie2[h, k]
            b[h, 4 + k] = net.push(mine, full2.at[h, k, k], then_dev(h, d))
    yield
    for h in range(2):
        for k in range(2, 6):
            b[h, k].wait_recv()
        out[h] = mid[h, :, then_at[h]] + full2[h, 0] + full2[h, 1]
    yield


def rows_of(parts, width):
    count = len(parts)
    rows = list(parts)
    if count < 8:
        rows.append(jnp.zeros((8 - count, width), F32))
    return jnp.concatenate(rows, axis=0)


def col_sum(t):
    return jnp.sum(t, axis=0, keepdims=True)


def body(
    views,
    gain,
    bias,
    w_hbm,
    loss,
    grad_weight,
    grad_gain,
    grad_bias,
    views_gradient,
    w,
    act,
    act_t,
    xhat,
    slope,
    stats,
    zacc,
    zbuf,
    zsum,
    zcb,
    colstat,
    kpart,
    krecv,
    ktie1,
    kfull1,
    kmid,
    ktie2,
    kfull2,
    kown,
    kgat,
    summed,
    gsum,
    dz,
    dgive,
    dkeep,
    drecv,
    dpart,
    dtie1,
    dfull1,
    dmid,
    dtie2,
    dfull2,
    dact,
    lsend,
    lrecv,
    fstat,
    send_sems,
    recv_sems,
    load_sem,
):
    net = Net(send_sems, recv_sems)
    z, y, x, core, chip = net.z, net.y, net.x, net.core, net.chip
    load = pltpu.make_async_copy(w_hbm, w, load_sem)
    load.start()
    barrier = pltpu.get_barrier_semaphore()
    peers = net.peers()
    for peer in peers:
        pl.semaphore_signal(barrier, inc=1, device_id=peer, device_id_type=MESH)
    local = []
    for v in range(2):
        t = views[v].astype(F32)
        m = col_sum(t) / 128.0
        local.append((m, col_sum((t - m) * (t - m))))
    stats[z] = rows_of([local[0][0], local[1][0], local[0][1], local[1][1]], 128)
    pl.semaphore_wait(barrier, len(peers))

    g = share_z(net, stats)
    next(g)
    next(g)
    inverse = []
    for v in range(2):
        m = stats[:, v, :]
        mean = col_sum(m) / PLANES
        spread = col_sum(stats[:, 2 + v, :] + 128.0 * (m - mean) * (m - mean))
        inv = 1.0 / jnp.sqrt(spread / ROWS + eps_norm)
        inverse.append(inv)
        xh = (views[v].astype(F32) - mean) * inv
        pre = gain[...] * xh + bias[...]
        inner = 0.7978845608028654 * (pre + 0.044715 * (pre * pre * pre))
        th = jnp.tanh(inner)
        a = 0.5 * pre * (1.0 + th)
        act[y, x, core, v] = a.astype(BF16).reshape(2, 4, 16, 128)
        xhat[v] = xh
        slope[v] = 0.5 * (1.0 + th) + 0.5 * pre * (1.0 - th * th) * (
            0.7978845608028654 * (1.0 + 3.0 * 0.044715 * (pre * pre))
        )

    for _ in gather_plane(net, act, True):
        pass

    row_v, row_s, row_q = lax.div(chip, 8), lax.rem(lax.div(chip, 4), 2), lax.rem(chip, 4)

    def feature_rows(plane):
        owner = plane * 2 + core
        return act.at[lax.div(owner, 4), lax.rem(owner, 4), :, row_v, row_s, row_q]

    own_rows = act_t.at[y, x, core, :, lax.div(z, 4), lax.rem(z, 4)]
    moved_rows = []
    for d in range(1, PLANES):
        moved_rows.append(net.push(feature_rows(mod8(z + d)), own_rows, net.at_z(d)))
    own_rows[...] = feature_rows(z)[...]

    load.wait()
    zacc[...] = jnp.zeros_like(zacc)

    def z_step(i, carry):
        cy, cx = lax.div(i, 4), lax.rem(i, 4)
        lhs = jnp.concatenate(
            [act[cy, cx, 0].reshape(256, 128), act[cy, cx, 1].reshape(256, 128)], axis=1
        )
        zacc[...] += dot_nn(lhs, w[pl.ds(pl.multiple_of(i * 256, 256), 256), :])
        return carry

    lax.fori_loop(0, 16, z_step, 0)
    zb = zacc[...].astype(BF16)
    zbuf[z] = zb.reshape(2, 128, 256)
    zf = zb.astype(F32)
    zsum[z] = rows_of([col_sum(zf[0:128]), col_sum(zf[128:256])], 256)

    means = share_z(net, zsum)
    next(means)
    zring = ring_z(net, zbuf)
    next(zring)
    for copy in moved_rows:
        copy.wait_recv()
    agt = gather_plane(net, act_t, True)
    next(agt)
    next(means)
    zmean = [col_sum(zsum[:, v, :]) / ROWS for v in range(2)]
    colstat[...] = jnp.zeros_like(colstat)

    def block_in(slot):
        for v in range(2):
            zc = zbuf[slot, v].astype(F32) - zmean[v]
            cb = zc.astype(BF16)
            zcb[slot, v] = cb
            cf = cb.astype(F32)
            colstat[v : v + 1, :] += col_sum(zc * zc)
            colstat[2 + v : 3 + v, :] += col_sum(cf * cf)
            kb = dot_nt(zcb[z, v], cb)
            kpart[lax.div(slot, 4), lax.rem(lax.div(slot, 2), 2), lax.rem(slot, 2), 2 * v : 2 * v + 2] = kb.reshape(
                2, 4, 16, 128
            )

    block_in(z)
    next(agt)
    next(zring)
    block_in(mod8(z + 7))
    block_in(mod8(z + 1))
    next(agt)
    next(zring)
    block_in(mod8(z + 6))
    block_in(mod8(z + 2))
    next(agt)
    next(zring)
    block_in(mod8(z + 5))
    block_in(mod8(z + 3))
    next(zring)
    block_in(mod8(z + 4))

    over = net.push(kpart.at[1 - core], krecv, net.partner())
    over.wait_recv()
    mine = kpart.at[core]
    mine[...] = mine[...] + krecv[...]
    for _ in reduce_plane(net, mine, ktie1, kfull1, kmid, ktie2, kfull2, kown):
        pass
    kgat[y, x, core] = kown[...].astype(BF16)
    gk = gather_plane(net, kgat, False)
    next(gk)
    next(agt)
    ksq = kown[...] * kown[...]
    ksq = col_sum(jnp.sum(ksq, axis=(0, 1)))
    for _ in gk:
        pass

    hinge_row = jnp.zeros((1, 256), F32)
    diag_row = jnp.zeros((1, 256), F32)
    local_sum = []
    for v in range(2):
        std = jnp.sqrt(colstat[v : v + 1, :] / (ROWS - 1) + eps_std)
        diag = colstat[2 + v : 3 + v, :]
        hinge_row = hinge_row + jnp.maximum(1.0 - std, 0.0)
        diag_row = diag_row + diag * diag
        moved = jnp.zeros((128, 256), F32)
        for b in range(0, 8, 2):
            lhs = jnp.concatenate(
                [
                    kgat[2 * v : 2 * v + 2, :, q // 4, (q // 2) % 2, q % 2].reshape(128, 128)
                    for q in (b, b + 1)
                ],
                axis=1,
            )
            rhs = jnp.concatenate([zcb[b, v], zcb[b + 1, v]], axis=0)
            moved = moved + dot_nn(lhs, rhs)
        zc = zbuf[z, v].astype(F32) - zmean[v]
        mask = jnp.where(std < 1.0, 1.0, 0.0)
        t = coef * (moved - zcb[z, v].astype(F32) * diag) - (hinge_coef * mask / std) * zc
        summed[v] = t
        local_sum.append(col_sum(t))
    gsum[z] = rows_of(local_sum, 256)
    totals = share_z(net, gsum)
    next(totals)
    diff = zbuf[z, 0].astype(F32) - zbuf[z, 1].astype(F32)
    inv_row = col_sum(diff * diff)
    wide = (25.0 / (ROWS * E)) * inv_row + (
        (25.0 / (2 * E)) * hinge_row - (1.0 / denom) * diag_row
    ) / PLANES
    share = wide[:, 0:128] + wide[:, 128:256] + (1.0 / denom) * ksq
    lsend[0] = rows_of([share], 128)
    loss_core = net.push(lsend.at[0], lrecv.at[0], net.partner())
    next(totals)
    for v in range(2):
        total = col_sum(gsum[:, v, :]) / ROWS
        sign = 1.0 if v == 0 else -1.0
        dz[z, v] = (summed[v] - total + (sign * inv_coef) * diff).astype(BF16).reshape(8, 16, 256)

    dring = ring_z(net, dz)
    next(dring)
    dzl = dz[z].reshape(256, 256)

    def dact_loop(store, parity):
        def step(i, carry):
            rows = w[pl.ds(pl.multiple_of((2 * i + parity) * 128, 128), 128), :]
            store[:, :, lax.div(i, 4), lax.rem(i, 4)] = dot_nt(dzl, rows).reshape(2, 2, 64, 128)
            return carry

        lax.fori_loop(0, 16, step, 0)

    dact_loop(dgive, 1 - core)
    over = [net.push(dgive.at[h], drecv.at[h], net.partner()) for h in range(2)]
    dact_loop(dkeep, core)
    for h in range(2):
        over[h].wait_recv()
        dpart[h] = (dkeep[h] + drecv[h]).astype(BF16)
    rs = reduce_plane(net, dpart, dtie1, dfull1, dmid, dtie2, dfull2, dact)
    next(rs)
    loss_core.wait_recv()
    lsend[1] = lsend[0] + lrecv[0]
    loss_x = [net.push(lsend.at[1], lrecv.at[d], net.at(y, mod4(x + d))) for d in range(1, 4)]
    next(dring)
    next(rs)
    next(dring)
    for copy in loss_x:
        copy.wait_recv()
    lsend[2] = lsend[1] + lrecv[1] + lrecv[2] + lrecv[3]
    loss_y = [net.push(lsend.at[2], lrecv.at[3 + d], net.at(mod4(y + d), x)) for d in range(1, 4)]
    next(rs)
    next(dring)
    next(rs)
    next(rs)
    for copy in loss_y:
        copy.wait_recv()
    plane_loss = lsend[2] + lrecv[4] + lrecv[5] + lrecv[6]

    sums = []
    for v in range(2):
        dp = dact[v].reshape(128, 128) * slope[v]
        dact[v] = dp.reshape(2, 64, 128)
        sums.append((col_sum(dp), col_sum(dp * xhat[v])))
    fstat[z] = rows_of([sums[0][0], sums[1][0], sums[0][1], sums[1][1], plane_loss[0:1]], 128)
    final = share_z(net, fstat)
    next(final)
    next(dring)

    def gw_step(i, carry):
        lhs, rhs = [], []
        for k in range(2):
            c = 2 * i + k
            cy, cx = lax.div(c, 4), lax.rem(c, 4)
            lhs.append(
                jnp.concatenate(
                    [act_t[cy, cx, q // 2, q % 2].reshape(128, 128) for q in range(4)], axis=1
                )
            )
            rhs.append(dz[:, lax.div(c, 8), lax.rem(c, 8)].reshape(128, 256))
        term = dot_tn(jnp.concatenate(lhs, axis=0), jnp.concatenate(rhs, axis=0))
        grad_weight[...] = jnp.where(i == 0, term, grad_weight[...] + term)
        return carry

    grad_weight[...] = jnp.zeros_like(grad_weight)
    lax.fori_loop(0, 8, gw_step, 0)
    next(final)
    total_b = [col_sum(fstat[:, v, :]) for v in range(2)]
    total_g = [col_sum(fstat[:, 2 + v, :]) for v in range(2)]
    grad_bias[...] = total_b[0] + total_b[1]
    grad_gain[...] = total_g[0] + total_g[1]
    loss[0, 0] = jnp.sum(fstat[:, 4, :])
    for v in range(2):
        dp = dact[v].reshape(128, 128)
        views_gradient[v] = (gain[...] * inverse[v]) * (
            dp - total_b[v] / ROWS - xhat[v] * (total_g[v] / ROWS)
        )
    for copy in net.sent:
        copy.wait_send()


MESSAGES = 280


def shards(views, norm_scale_gain, norm_shift_bias, weight):
    vmem = pltpu.VMEM

    def reducer(n, dtype):
        return [
            vmem((2, 2, 2, 2, n, 128), dtype),
            vmem((2, 2, 2, 4, n, 128), dtype),
            vmem((2, 2, 4, n, 128), F32),
            vmem((2, 2, n, 128), F32),
            vmem((2, 2, 2, n, 128), F32),
            vmem((2, 2, n, 128), F32),
        ]

    scratch = [
        vmem((4096, 256), BF16),
        vmem((4, 4, 2, 2, 2, 4, 16, 128), BF16),
        vmem((4, 4, 2, 2, 2, 4, 16, 128), BF16),
        vmem((2, 128, 128), F32),
        vmem((2, 128, 128), F32),
        vmem((8, 8, 128), F32),
        vmem((256, 256), F32),
        vmem((8, 2, 128, 256), BF16),
        vmem((8, 8, 256), F32),
        vmem((8, 2, 128, 256), BF16),
        vmem((8, 256), F32),
        vmem((2, 2, 2, 4, 4, 16, 128), F32),
        vmem((2, 2, 4, 4, 16, 128), F32),
        *reducer(16, F32),
        vmem((4, 4, 2, 2, 2, 16, 128), BF16),
        vmem((2, 128, 256), F32),
        vmem((8, 8, 256), F32),
        vmem((8, 2, 8, 16, 256), BF16),
        vmem((2, 2, 4, 4, 64, 128), F32),
        vmem((2, 2, 4, 4, 64, 128), F32),
        vmem((2, 2, 4, 4, 64, 128), F32),
        vmem((2, 2, 4, 4, 64, 128), BF16),
        *reducer(64, BF16),
        vmem((3, 8, 128), F32),
        vmem((7, 8, 128), F32),
        vmem((8, 8, 128), F32),
        pltpu.SemaphoreType.DMA((MESSAGES,)),
        pltpu.SemaphoreType.DMA((MESSAGES,)),
        pltpu.SemaphoreType.DMA,
    ]
    whole = pl.BlockSpec(memory_space=pltpu.VMEM)
    loss, grad_weight, grad_gain, grad_bias, views_gradient = pl.pallas_call(
        body,
        out_shape=(
            jax.ShapeDtypeStruct((1, 1), F32),
            jax.ShapeDtypeStruct((512, 256), F32),
            jax.ShapeDtypeStruct((1, 128), F32),
            jax.ShapeDtypeStruct((1, 128), F32),
            jax.ShapeDtypeStruct((2, 128, 128), F32),
        ),
        in_specs=[whole, whole, whole, pl.BlockSpec(memory_space=pl.ANY)],
        out_specs=(pl.BlockSpec(memory_space=pltpu.SMEM), whole, whole, whole, whole),
        scratch_shapes=scratch,
        compiler_params=pltpu.CompilerParams(collective_id=0, has_side_effects=True),
        name="vicreg_step",
    )(views, norm_scale_gain.reshape(1, 128), norm_shift_bias.reshape(1, 128), weight)
    return (
        loss.reshape(()),
        grad_weight,
        grad_gain.reshape(128),
        grad_bias.reshape(128),
        views_gradient,
    )


def solution(mesh):
    placed = (P(None, "batch", "col"), P("col"), P("col"), P(None, "col"))
    return jax.shard_map(
        shards,
        mesh=mesh,
        in_specs=placed,
        out_specs=(P(), P("batch", "col"), P("col"), P("col"), P(None, "batch", "col")),
        check_vma=False,
    )
```

time: 431 us -> 122 us (0.28)
  waiting for transfers between devices: 241 us -> 0 us
  blocking collectives: 142 us -> 0 us
  Pallas kernels: 0 us -> 113 us
  other arithmetic: 14.9 us -> 0 us
  between operations: 16.5 us -> 2.39 us
  matrix products: 13.8 us -> 0 us
  local copies, waits for them, and re-layouts: 1.38 us -> 5.69 us
    psum x5 -> x0, blocking collectives: 142 us -> none  [the longest x1 72.5 us: shards(): loss = lax.psum(share, ('batch', 'col'))]
    pallas_call x0 -> x1, Pallas kernels: none -> 113 us  [shards(): pl.pallas_call(body, out_shape=(jax.ShapeDtypeStruct((1, 1), F32), jax.Sh...]
    psum x1 -> x0, waiting for transfers between devices: 110 us -> none  [shards(): kernel = lax.psum(kernel_part, 'col')]
    all_gather x2 -> x0, waiting for transfers between devices: 87.3 us -> none  [the longest x1 48.6 us: shards(): act_full = lax.all_gather(act, 'col', axis=2, tiled=True)]
    reduce_scatter x2 -> x0, waiting for transfers between devices: 43.6 us -> none  [the longest x1 37.9 us: shards(): lax.psum_scatter(jnp.einsum('vrk,vrj->kj', act_full, dzb, preferred_eleme...]
    dot_general x5 -> x0, matrix products: 13.8 us -> none  [the longest x1 4.29 us: shards(): jnp.einsum('vrk,vrj->kj', act_full, dzb, preferred_element_type=jnp.float32)]
    reduce_sum x8 -> x0, other arithmetic: 8.51 us -> none  [the longest x1 2.09 us: shards(): jnp.sum(jnp.square(zcb_all.astype(jnp.float32)), axis=1, keepdims=True)]
    unnamed x16 -> x4, local copies, waits for them, and re-layouts: 1.38 us -> 5.69 us
  transfers between devices with their start and end apart: 5 -> 0, of which waited for: 5 -> 0; matrix products, arithmetic and copies ran while one was open for 3% -> 0% of each run, Pallas kernels for 0% -> 0%
where the time goes in v1:
time: 122 us; the launch traced here: 121 us
  Pallas kernels  113 us (93%)
  local copies, waits for them, and re-layouts  5.69 us (5%)
  between operations  2.39 us (2%)
    pallas_call x1, Pallas kernels, shards(): pl.pallas_call(body, out_shape=(jax.ShapeDtypeStruct((1, 1), F32), jax.Sh...  113 us
    unnamed x4, local copies, waits for them, and re-layouts  5.69 us

profile of v1, /device:TPU:8, one launch (start us, length us, event | category | flops | bytes accessed | tf_op | source)
XLA Modules:
  0.0 121.2 jit_solution(16285391392012518391)
XLA Ops:
  0.6 113.1 %vicreg_step.1 = (f32[1,1]{1,0:T(1,128)}, f32[512,256]{1,0:T(8,128)}, f32[1,128]{1,0:T(1,128)}, f32[1,128]{1,0:T(1,128)}, f32[2,128,128]{2,1,0:T(8,128)}) custom-call(bf16[2,128,128]{2,1,0:T(8,128)(2,1)} %views.1, f32[1,128]{1,0:T(1,128)} %bitcast.5, f32[1,128]{1,0:T(1,128)} %bitcast.6, bf16[4096,256]{1,0:T(8,128)(2,1)} %w_hbm.1), custom_call_target="tpu_custom_call" | custom-call | tf_op jit(solution)/shard_map/vicreg_step/pallas_call | solution.py:613
  114.4 1.9 %copy.15 = f32[512,256]{1,0:T(8,128)} copy(f32[512,256]{1,0:T(8,128)} %get-tuple-element.21) | data formatting | bytes 1048576
  116.2 1.1 copy.16
  117.4 1.1 copy.17
  118.5 1.6 %copy.18 = f32[2,128,128]{2,1,0:T(8,128)} copy(f32[2,128,128]{2,1,0:T(8,128)} %get-tuple-element.24) | data formatting | bytes 262144

commit v2 on v0

v2 whole, which is shorter than its diff:
```python
import jax
import jax.numpy as jnp
from jax import lax
from jax.experimental import pallas as pl
from jax.experimental.pallas import tpu as pltpu
from jax.sharding import PartitionSpec as P

E = 8192
ROWS = 1024
PLANES = 8
SIDE = 4

eps_norm = 1e-05
eps_std = 0.0001
scale = ROWS * E / 128.0
denom = float((ROWS - 1) ** 2 * E)
coef = 4.0 * scale / denom
hinge_coef = 25.0 * scale / (2.0 * E * (ROWS - 1))
inv_coef = 50.0 * scale / (ROWS * E)

F32 = jnp.float32
BF16 = jnp.bfloat16
MESH = pl.DeviceIdType.MESH


def dot_nt(a, b):
    return lax.dot_general(a, b, (((1,), (1,)), ((), ())), preferred_element_type=F32)


def dot_tn(a, b):
    return lax.dot_general(a, b, (((0,), (0,)), ((), ())), preferred_element_type=F32)


def dot_nn(a, b):
    return jnp.dot(a, b, preferred_element_type=F32)


class Net:
    def __init__(self, send, recv):
        self.send, self.recv, self.used, self.open = send, recv, 0, []
        self.z = lax.axis_index("batch")
        self.c = lax.axis_index("col")
        self.core = lax.rem(self.c, 2)
        self.chip = lax.div(self.c, 2)
        self.x = lax.rem(self.chip, SIDE)
        self.y = lax.div(self.chip, SIDE)

    def at_z(self, d):
        return (mod8(self.z + d), self.c)

    def at(self, y, x):
        return (self.z, (y * SIDE + x) * 2 + self.core)

    def along(self, h, f, t):
        return self.at(t, f) if h == 0 else self.at(f, t)

    def partner(self):
        return (self.z, self.chip * 2 + 1 - self.core)

    def copy(self, src, dst, device, i):
        return pltpu.make_async_remote_copy(
            src_ref=src,
            dst_ref=dst,
            send_sem=self.send.at[i],
            recv_sem=self.recv.at[i],
            device_id=device,
            device_id_type=MESH,
        )

    def group(self, meter):
        i = self.used
        self.used += 1
        whole = self.copy(meter, meter, self.partner(), i)
        self.open.append(whole)
        return i, whole

    def push(self, src, dst, device, group=None):
        if group is not None:
            self.copy(src, dst, device, group[0]).start()
            return None
        i = self.used
        self.used += 1
        one = self.copy(src, dst, device, i)
        one.start()
        self.open.append(one)
        return one

    def peers(self):
        found = [self.partner()]
        found += [self.at_z(d) for d in range(1, PLANES)]
        found += [self.at(mod4(self.y + dy), mod4(self.x + dx)) for dy, dx in OFFSETS]
        return found


OFFSETS = [(dy, dx) for dy in (2, 1, 3, 0) for dx in (2, 1, 3, 0) if (dy, dx) != (0, 0)]


def mod4(a):
    return lax.rem(a, SIDE)


def mod8(a):
    return lax.rem(a, PLANES)


def share_z(net, buf):
    group = net.group(buf.at[0:7])
    for d in (4, 3, 5, 2, 6, 1, 7):
        net.push(buf.at[net.z], buf.at[net.z], net.at_z(d), group)
    yield
    group[1].wait_recv()
    yield


def share_plane(net, src, dst):
    group = net.group(dst)
    for k, (dy, dx) in enumerate(OFFSETS):
        net.push(src, dst.at[k], net.at(mod4(net.y + dy), mod4(net.x + dx)), group)
    return group[1]


def ring_z(net, buf):
    up, down = {}, {}
    for q in range(4):
        own = buf.at[net.z, q]
        up[1, q] = net.push(own, own, net.at_z(1))
        down[1, q] = net.push(own, own, net.at_z(7))
    yield
    for d in range(1, 5):
        for q in range(4):
            if d < 4 or q < 2:
                up[d, q].wait_recv()
                if d < 3 or (d == 3 and q < 2):
                    block = buf.at[mod8(net.z + 8 - d), q]
                    up[d + 1, q] = net.push(block, block, net.at_z(1))
            if d < 4 or q >= 2:
                down[d, q].wait_recv()
                if d < 3 or (d == 3 and q >= 2):
                    block = buf.at[mod8(net.z + d), q]
                    down[d + 1, q] = net.push(block, block, net.at_z(7))
            if q == 1 and d < 4:
                yield
        yield


def gather_plane(net, buf):
    first_at, then_at = (net.x, net.y), (net.y, net.x)
    shift = (0, 3, 1, 2)
    first, cross, over = {}, {}, {}

    def piece(h, f, t):
        y, x = (t, f) if h == 0 else (f, t)
        return buf.at[y, x, net.core, h]

    def spread(h, j):
        f = mod4(first_at[h] + shift[j])
        cross[h, j] = net.group(buf.at[0:3, 0, 0, 0])
        block = piece(h, f, then_at[h])
        for d in (2, 1, 3):
            net.push(block, block, net.along(h, f_own[h], mod4(then_at[h] + d)), cross[h, j])

    def hand_over(h, j):
        cross[h, j][1].wait_recv()
        f = mod4(first_at[h] + shift[j])
        line = buf.at[:, f, net.core, 0] if h == 0 else buf.at[f, :, net.core, 1]
        over[h, j] = net.push(line, line, net.partner())

    f_own = first_at
    for h in range(2):
        block = piece(h, first_at[h], then_at[h])
        for d in (1, 3, 2):
            first[h, d] = net.push(block, block, net.along(h, mod4(first_at[h] + d), then_at[h]))
    for h in range(2):
        spread(h, 0)
    yield
    for j, d in ((1, 1), (2, 3), (3, 2)):
        for h in range(2):
            first[h, d].wait_recv()
            spread(h, j)
    yield
    for j in range(4):
        for h in range(2):
            hand_over(h, j)
        yield
        if j > 0:
            for h in range(2):
                over[h, j - 1].wait_recv()
            yield
    for h in range(2):
        over[h, 3].wait_recv()
    yield


def rows_of(parts, width):
    count = len(parts)
    rows = list(parts)
    if count < 8:
        rows.append(jnp.zeros((8 - count, width), F32))
    return jnp.concatenate(rows, axis=0)


def col_sum(t):
    return jnp.sum(t, axis=0, keepdims=True)


def split3(t):
    hi = t.astype(BF16)
    rest = t - hi.astype(F32)
    mid = rest.astype(BF16)
    lo = (rest - mid.astype(F32)).astype(BF16)
    zero = jnp.zeros((5, t.shape[1]), F32)
    return jnp.concatenate([hi.astype(F32), mid.astype(F32), lo.astype(F32), zero], axis=0).astype(BF16)


STAGES = ((1, 7), (2, 6), (3, 5), (0, 4))


def body(
    views,
    gain,
    bias,
    w_hbm,
    grad_weight,
    small,
    views_gradient,
    w,
    act,
    act_t,
    xhat,
    slope,
    stats,
    zacc,
    zbuf,
    zsum,
    zcb,
    colstat,
    kpart,
    krecv,
    kmine,
    kin,
    kown,
    kgat,
    rsum,
    rcore,
    rmine,
    rin,
    moved,
    dz,
    dgive,
    dkeep,
    drecv,
    dpart,
    din,
    dmid,
    dmid_in,
    dpre,
    lsend,
    lrecv,
    fstat,
    send_sems,
    recv_sems,
    load_sem,
):
    net = Net(send_sems, recv_sems)
    z, y, x, core, chip = net.z, net.y, net.x, net.core, net.chip
    load = pltpu.make_async_copy(w_hbm, w, load_sem)
    load.start()
    barrier = pltpu.get_barrier_semaphore()
    peers = net.peers()
    for peer in peers:
        pl.semaphore_signal(barrier, inc=1, device_id=peer, device_id_type=MESH)
    local = []
    for v in range(2):
        t = views[v].astype(F32)
        m = col_sum(t) / 128.0
        local.append((m, col_sum((t - m) * (t - m))))
    stats[z] = rows_of([local[0][0], local[1][0], local[0][1], local[1][1]], 128)
    pl.semaphore_wait(barrier, len(peers))

    g = share_z(net, stats)
    next(g)
    next(g)
    inverse = []
    for v in range(2):
        m = stats[:, v, :]
        mean = col_sum(m) / PLANES
        spread = col_sum(stats[:, 2 + v, :] + 128.0 * (m - mean) * (m - mean))
        inv = 1.0 / jnp.sqrt(spread / ROWS + eps_norm)
        inverse.append(inv)
        xh = (views[v].astype(F32) - mean) * inv
        pre = gain[...] * xh + bias[...]
        inner = 0.7978845608028654 * (pre + 0.044715 * (pre * pre * pre))
        th = jnp.tanh(inner)
        a = 0.5 * pre * (1.0 + th)
        act[y, x, core, v] = a.astype(BF16).reshape(2, 4, 16, 128)
        xhat[v] = xh
        slope[v] = 0.5 * (1.0 + th) + 0.5 * pre * (1.0 - th * th) * (
            0.7978845608028654 * (1.0 + 3.0 * 0.044715 * (pre * pre))
        )

    def z_terms(j):
        for h in range(2):
            if h == 0:
                f = mod4(x + (0, 3, 1, 2)[j])
                lhs = [act[k, f, q, 0].reshape(128, 128) for k in range(4) for q in range(2)]
                rhs = w[:, f].reshape(1024, 256)
            else:
                f = mod4(y + (0, 3, 1, 2)[j])
                lhs = [act[f, k, q, 1].reshape(128, 128) for k in range(4) for q in range(2)]
                rhs = w[f].reshape(1024, 256)
            term = dot_nn(jnp.concatenate(lhs, axis=1), rhs)
            if j == 0:
                zacc[h] = term
            else:
                zacc[h] = zacc[h] + term

    ag = gather_plane(net, act)
    next(ag)
    next(ag)
    next(ag)
    load.wait()
    for j in range(3):
        next(ag)
        next(ag)
        z_terms(j)
    next(ag)

    row_v, row_s, row_q = lax.div(chip, 8), lax.rem(lax.div(chip, 4), 2), lax.rem(chip, 4)

    def feature_rows(plane):
        owner = plane * 2 + core
        return act.at[lax.div(owner, 4), lax.rem(owner, 4), :, row_v, row_s, row_q]

    z_terms(3)
    zb = zacc[...].astype(BF16)
    zbuf[z] = zb.reshape(4, 64, 256)
    zf = zb.astype(F32)
    zsum[z] = rows_of([col_sum(zf[0]), col_sum(zf[1])], 256)
    means = share_z(net, zsum)
    next(means)
    zring = ring_z(net, zbuf)
    next(zring)
    own_rows = act_t.at[y, x, core, :, lax.div(z, 4), lax.rem(z, 4)]
    features = [
        net.push(feature_rows(mod8(z + d)), own_rows, net.at_z(d)) for d in range(1, PLANES)
    ]
    own_rows[...] = feature_rows(z)[...]
    colstat[...] = jnp.zeros_like(colstat)

    def block_in(stage, owner, v):
        slot = mod8(z + STAGES[stage][owner])
        zc = zbuf[slot, 2 * v : 2 * v + 2].reshape(128, 256).astype(F32) - zmean[v]
        cb = zc.astype(BF16)
        zcb[slot, v] = cb
        cf = cb.astype(F32)
        colstat[v : v + 1, :] += col_sum(zc * zc)
        colstat[2 + v : 3 + v, :] += col_sum(cf * cf)
        colstat[4 + v : 5 + v, :] += col_sum(cf)
        colstat[6 + v : 7 + v, :] += col_sum(zc)
        kpart[stage, owner, 8 * v : 8 * v + 8] = dot_nt(zcb[z, v], cb).reshape(8, 16, 128)

    k_over, k_in, k_gat, k_done = {}, {}, {}, {}

    def k_give(stage):
        k_over[stage] = net.push(kpart.at[stage, 1 - core], krecv.at[stage], net.partner())

    def k_spread(stage):
        k_over[stage].wait_recv()
        kmine[stage] = kpart[stage, core] + krecv[stage]
        group = net.group(kin.at[stage])
        for k, (dy, dx) in enumerate(OFFSETS):
            ty, tx = mod4(y + dy), mod4(x + dx)
            net.push(kmine.at[stage, ty * SIDE + tx], kin.at[stage, k], net.at(ty, tx), group)
        k_in[stage] = group[1]

    def k_gather(stage):
        k_in[stage].wait_recv()
        total = kmine[stage, chip] + jnp.sum(kin[stage], axis=0)
        kown[stage] = total
        kgat[stage, core, chip] = total.astype(BF16)
        own = kgat.at[stage, core, chip]
        group = net.group(kgat.at[stage, core, 0:15])
        for dy, dx in OFFSETS:
            net.push(own, own, net.at(mod4(y + dy), mod4(x + dx)), group)
        k_gat[stage] = group[1]

    def k_hand(stage):
        k_gat[stage].wait_recv()
        k_done[stage] = net.push(kgat.at[stage, core], kgat.at[stage, core], net.partner())

    def k_moved(stage):
        k_done[stage].wait_recv()
        slots = [mod8(z + r) for r in STAGES[stage]]
        for v in range(2):
            lhs = jnp.concatenate(
                [kgat[stage, q, 8 * v : 8 * v + 8].reshape(128, 128) for q in range(2)], axis=1
            )
            rhs = jnp.concatenate([zcb[slots[0], v], zcb[slots[1], v]], axis=0)
            term = dot_nn(lhs, rhs)
            if stage == 0:
                moved[v] = term
            else:
                moved[v] = moved[v] + term

    next(zring)
    for copy in features:
        copy.wait_recv()
    agt = gather_plane(net, act_t)
    next(agt)
    next(zring)
    next(means)
    zmean = [col_sum(zsum[:, v, :]) / ROWS for v in range(2)]
    for v in range(2):
        block_in(3, 0, v)
    for v in range(2):
        block_in(0, 0, v)
        block_in(0, 1, v)
    k_give(0)
    next(zring)
    k_spread(0)
    next(agt)
    next(zring)
    for v in range(2):
        block_in(1, 0, v)
        block_in(1, 1, v)
    k_give(1)
    next(zring)
    k_gather(0)
    k_spread(1)
    next(zring)
    for v in range(2):
        block_in(2, 0, v)
        block_in(2, 1, v)
    k_give(2)
    next(zring)
    for v in range(2):
        block_in(3, 1, v)
    k_give(3)
    k_spread(2)

    total_rows = [split3(colstat[4 + v : 5 + v, :]) for v in range(2)]
    for v in range(2):
        for slot in range(PLANES):
            rsum[v * PLANES + slot : v * PLANES + slot + 1, :] = col_sum(
                dot_nt(total_rows[v], zcb[slot, v])
            )
    r_over = net.push(rsum, rcore, net.partner())
    k_spread(3)
    k_gather(1)
    r_over.wait_recv()
    rmine[...] = rsum[...] + rcore[...]
    r_in = share_plane(net, rmine, rin)
    k_gather(2)
    k_hand(0)
    next(agt)
    k_gather(3)
    k_hand(1)
    k_moved(0)
    k_hand(2)
    k_moved(1)
    r_in.wait_recv()
    row_total = rmine[...] + jnp.sum(rin[...], axis=0)
    k_hand(3)
    k_moved(2)
    next(agt)
    next(agt)
    next(agt)
    next(agt)
    next(agt)
    next(agt)
    std, diag, mean_t = [], [], []
    for v in range(2):
        std.append(jnp.sqrt(colstat[v : v + 1, :] / (ROWS - 1) + eps_std))
        diag.append(colstat[2 + v : 3 + v, :])
        m = jnp.zeros((8, 256), F32)
        for slot in range(PLANES):
            r = v * PLANES + slot
            m = m + dot_nn(split3(row_total[r : r + 1, :]), zcb[slot, v])
        hinge = jnp.where(std[v] < 1.0, hinge_coef, 0.0) / std[v]
        mean_t.append(
            (
                coef * (col_sum(m) - diag[v] * colstat[4 + v : 5 + v, :])
                - hinge * colstat[6 + v : 7 + v, :]
            )
            / ROWS
        )
    k_moved(3)
    zl = [zbuf[z, 2 * v : 2 * v + 2].reshape(128, 256).astype(F32) for v in range(2)]
    diff = zl[0] - zl[1]
    for v in range(2):
        hinge = jnp.where(std[v] < 1.0, hinge_coef, 0.0) / std[v]
        t = coef * (moved[v] - zcb[z, v].astype(F32) * diag[v]) - hinge * (zl[v] - zmean[v])
        sign = 1.0 if v == 0 else -1.0
        d = (t - mean_t[v] + (sign * inv_coef) * diff).astype(BF16)
        dz[z, 2 * v : 2 * v + 2] = d.reshape(2, 4, 16, 256)

    dring = ring_z(net, dz)
    next(dring)
    first_at, then_at = (x, y), (y, x)
    dzl = [dz[z, 2 * v : 2 * v + 2].reshape(128, 256) for v in range(2)]
    d_over, d_in, d_mid = {}, {}, {}

    def d_terms(h, g, parity, store):
        f = mod4(first_at[h] + g)
        rows = w[:, f, parity] if h == 0 else w[f, :, parity]
        t = dot_nt(dzl[h], rows.reshape(512, 256))
        for k in range(4):
            store[h, g, k] = t[:, 128 * k : 128 * k + 128]

    def d_send(h, g):
        d_over[h, g].wait_recv()
        if g == 0:
            return
        dpart[h, g] = (dkeep[h, g] + drecv[h, g]).astype(BF16)
        f = mod4(first_at[h] + g)
        d_in[h, g] = net.push(dpart.at[h, g], din.at[h, g], net.along(h, f, then_at[h]))

    last = None
    for g in (2, 1, 3, 0):
        for h in range(2):
            d_terms(h, g, 1 - core, dgive)
            d_over[h, g] = net.push(dgive.at[h, g], drecv.at[h, g], net.partner())
        for h in range(2):
            d_terms(h, g, core, dkeep)
        if last is not None:
            for h in range(2):
                d_send(h, last)
        last = g
    next(dring)
    for h in range(2):
        d_send(h, 0)

    inv_row = col_sum(diff * diff)
    hinge_row = jnp.maximum(1.0 - std[0], 0.0) + jnp.maximum(1.0 - std[1], 0.0)
    diag_row = diag[0] * diag[0] + diag[1] * diag[1]
    wide = (25.0 / (ROWS * E)) * inv_row + (
        (25.0 / (2 * E)) * hinge_row - (1.0 / denom) * diag_row
    ) / PLANES
    ksq = col_sum(jnp.sum(kown[...] * kown[...], axis=0))
    share = wide[:, 0:128] + wide[:, 128:256] + (1.0 / denom) * ksq
    lsend[0] = rows_of([share], 128)
    loss_core = net.push(lsend.at[0], lrecv.at[15], net.partner())
    next(dring)
    next(dring)
    loss_core.wait_recv()
    lsend[1] = lsend[0] + lrecv[15]
    loss_in = share_plane(net, lsend.at[1], lrecv.at[0:15])
    for h in range(2):
        for g in range(1, 4):
            d_in[h, g].wait_recv()
        dmid[h] = dkeep[h, 0] + drecv[h, 0] + (
            din[h, 1].astype(F32) + din[h, 2].astype(F32) + din[h, 3].astype(F32)
        )
        group = net.group(dmid_in.at[h])
        for k, d in enumerate((2, 1, 3)):
            t = mod4(then_at[h] + d)
            net.push(dmid.at[h, t], dmid_in.at[h, k], net.along(h, first_at[h], t), group)
        d_mid[h] = group[1]
    next(dring)
    next(dring)
    loss_in.wait_recv()
    plane_loss = lsend[1, 0:1, :] + jnp.sum(lrecv[0:15, 0:1, :], axis=0)
    next(dring)
    sums = []
    for h in range(2):
        d_mid[h].wait_recv()
        d_act = dmid[h, then_at[h]] + dmid_in[h, 0] + dmid_in[h, 1] + dmid_in[h, 2]
        dp = d_act * slope[h]
        dpre[h] = dp
        sums.append((col_sum(dp), col_sum(dp * xhat[h])))
    fstat[z] = rows_of([sums[0][0], sums[1][0], sums[0][1], sums[1][1], plane_loss], 128)
    final = share_z(net, fstat)
    next(final)
    next(dring)
    next(agt)

    def gw_step(i, carry):
        lhs, rhs = [], []
        for k in range(2):
            c = 2 * i + k
            cy, cx = lax.div(c, 4), lax.rem(c, 4)
            lhs.append(
                jnp.concatenate(
                    [act_t[cy, cx, q // 2, q % 2].reshape(128, 128) for q in range(4)], axis=1
                )
            )
            rhs.append(dz[:, cy, cx].reshape(128, 256))
        term = dot_tn(jnp.concatenate(lhs, axis=0), jnp.concatenate(rhs, axis=0))
        grad_weight[...] = jnp.where(i == 0, term, grad_weight[...] + term)
        return carry

    grad_weight[...] = jnp.zeros_like(grad_weight)
    lax.fori_loop(0, 8, gw_step, 0)
    next(final)
    total_b = [col_sum(fstat[:, v, :]) for v in range(2)]
    total_g = [col_sum(fstat[:, 2 + v, :]) for v in range(2)]
    small[...] = rows_of([total_g[0] + total_g[1], total_b[0] + total_b[1], col_sum(fstat[:, 4, :])], 128)
    for v in range(2):
        views_gradient[v] = (gain[...] * inverse[v]) * (
            dpre[v] - total_b[v] / ROWS - xhat[v] * (total_g[v] / ROWS)
        )
    for copy in net.open:
        copy.wait_send()


MESSAGES = 150


def finish(gw_in, small, vg_in, loss, grad_weight, grad_gain, grad_bias, views_gradient):
    grad_weight[...] = gw_in[...]
    views_gradient[...] = vg_in[...]
    grad_gain[...] = small[0:1, :]
    grad_bias[...] = small[1:2, :]
    loss[0, 0] = jnp.sum(small[2:3, :])


def shards(views, norm_scale_gain, norm_shift_bias, weight):
    vmem = pltpu.VMEM
    scratch = [
        vmem((4, 4, 2, 128, 256), BF16),
        vmem((4, 4, 2, 2, 2, 4, 16, 128), BF16),
        vmem((4, 4, 2, 2, 2, 4, 16, 128), BF16),
        vmem((2, 128, 128), F32),
        vmem((2, 128, 128), F32),
        vmem((8, 8, 128), F32),
        vmem((2, 128, 256), F32),
        vmem((8, 4, 64, 256), BF16),
        vmem((8, 8, 256), F32),
        vmem((8, 2, 128, 256), BF16),
        vmem((8, 256), F32),
        vmem((4, 2, 16, 16, 128), F32),
        vmem((4, 16, 16, 128), F32),
        vmem((4, 16, 16, 128), F32),
        vmem((4, 15, 16, 128), F32),
        vmem((4, 16, 128), F32),
        vmem((4, 2, 16, 16, 128), BF16),
        vmem((16, 128), F32),
        vmem((16, 128), F32),
        vmem((16, 128), F32),
        vmem((15, 16, 128), F32),
        vmem((2, 128, 256), F32),
        vmem((8, 4, 4, 16, 256), BF16),
        vmem((2, 4, 4, 128, 128), F32),
        vmem((2, 4, 4, 128, 128), F32),
        vmem((2, 4, 4, 128, 128), F32),
        vmem((2, 4, 4, 128, 128), BF16),
        vmem((2, 4, 4, 128, 128), BF16),
        vmem((2, 4, 128, 128), F32),
        vmem((2, 3, 128, 128), F32),
        vmem((2, 128, 128), F32),
        vmem((2, 8, 128), F32),
        vmem((16, 8, 128), F32),
        vmem((8, 8, 128), F32),
        pltpu.SemaphoreType.DMA((MESSAGES,)),
        pltpu.SemaphoreType.DMA((MESSAGES,)),
        pltpu.SemaphoreType.DMA,
    ]
    whole = pl.BlockSpec(memory_space=pltpu.VMEM)
    made = (
        jax.ShapeDtypeStruct((512, 256), F32),
        jax.ShapeDtypeStruct((8, 128), F32),
        jax.ShapeDtypeStruct((2, 128, 128), F32),
    )
    results = pl.pallas_call(
        body,
        out_shape=made,
        in_specs=[whole, whole, whole, pl.BlockSpec(memory_space=pl.ANY)],
        out_specs=(whole, whole, whole),
        scratch_shapes=scratch,
        compiler_params=pltpu.CompilerParams(collective_id=0, has_side_effects=True),
        name="vicreg_step",
    )(
        views,
        norm_scale_gain.reshape(1, 128),
        norm_shift_bias.reshape(1, 128),
        weight.reshape(4, 4, 2, 128, 256),
    )
    loss, grad_weight, grad_gain, grad_bias, views_gradient = pl.pallas_call(
        finish,
        out_shape=(
            jax.ShapeDtypeStruct((1, 1), F32),
            made[0],
            jax.ShapeDtypeStruct((1, 128), F32),
            jax.ShapeDtypeStruct((1, 128), F32),
            made[2],
        ),
        in_specs=[whole, whole, whole],
        out_specs=(pl.BlockSpec(memory_space=pltpu.SMEM), whole, whole, whole, whole),
        name="write_results",
    )(*results)
    return (
        loss.reshape(()),
        grad_weight,
        grad_gain.reshape(128),
        grad_bias.reshape(128),
        views_gradient,
    )


def solution(mesh):
    placed = (P(None, "batch", "col"), P("col"), P("col"), P(None, "col"))
    return jax.shard_map(
        shards,
        mesh=mesh,
        in_specs=placed,
        out_specs=(P(), P("batch", "col"), P("col"), P("col"), P(None, "batch", "col")),
        check_vma=False,
    )
```

time: 431 us -> 87.3 us (0.20)
  waiting for transfers between devices: 241 us -> 0 us
  blocking collectives: 142 us -> 0 us
  Pallas kernels: 0 us -> 85.9 us
  between operations: 16.5 us -> 0.64 us
  other arithmetic: 14.9 us -> 0 us
  matrix products: 13.8 us -> 0 us
    psum x5 -> x0, blocking collectives: 142 us -> none  [the longest x1 72.5 us: shards(): loss = lax.psum(share, ('batch', 'col'))]
    psum x1 -> x0, waiting for transfers between devices: 110 us -> none  [shards(): kernel = lax.psum(kernel_part, 'col')]
    all_gather x2 -> x0, waiting for transfers between devices: 87.3 us -> none  [the longest x1 48.6 us: shards(): act_full = lax.all_gather(act, 'col', axis=2, tiled=True)]
    pallas_call x0 -> x2, Pallas kernels: none -> 85.9 us  [the longest x1 83.9 us: shards(): pl.pallas_call(body, out_shape=made, in_specs=[whole, whole, whole, pl.Bl...]
    reduce_scatter x2 -> x0, waiting for transfers between devices: 43.6 us -> none  [the longest x1 37.9 us: shards(): lax.psum_scatter(jnp.einsum('vrk,vrj->kj', act_full, dzb, preferred_eleme...]
    dot_general x5 -> x0, matrix products: 13.8 us -> none  [the longest x1 4.29 us: shards(): jnp.einsum('vrk,vrj->kj', act_full, dzb, preferred_element_type=jnp.float32)]
    reduce_sum x8 -> x0, other arithmetic: 8.51 us -> none  [the longest x1 2.09 us: shards(): jnp.sum(jnp.square(zcb_all.astype(jnp.float32)), axis=1, keepdims=True)]
  transfers between devices with their start and end apart: 5 -> 0, of which waited for: 5 -> 0; matrix products, arithmetic and copies ran while one was open for 3% -> 0% of each run, Pallas kernels for 0% -> 0%
where the time goes in v2:
time: 87.3 us; the launch traced here: 86.5 us
  Pallas kernels  85.9 us (98%)
    pallas_call x1, Pallas kernels, shards(): pl.pallas_call(body, out_shape=made, in_specs=[whole, whole, whole, pl.Bl...  83.9 us
    pallas_call x1, Pallas kernels, shards(): pl.pallas_call(finish, out_shape=(jax.ShapeDtypeStruct((1, 1), F32), made...  1.94 us

profile of v2, /device:TPU:8, one launch (start us, length us, event | category | flops | bytes accessed | tf_op | source)
XLA Modules:
  0.0 86.5 jit_solution(5267114907209494380)
XLA Ops:
  0.6 83.9 %vicreg_step.1 = (f32[512,256]{1,0:T(8,128)}, f32[8,128]{1,0:T(8,128)}, f32[2,128,128]{2,1,0:T(8,128)}) custom-call(bf16[2,128,128]{2,1,0:T(8,128)(2,1)} %views.1, f32[1,128]{1,0:T(1,128)} %bitcast.7, f32[1,128]{1,0:T(1,128)} %bitcast.8, bf16[4,4,2,128,256]{4,3,2,1,0:T(8,128)(2,1)} %bitcast.6), custom_call_target="tpu_custom_call" | custom-call | tf_op jit(solution)/shard_map/vicreg_step/pallas_call | solution.py:664
  84.6 1.9 %write_results.1 = (f32[1,1]{1,0:T(1,128)}, f32[512,256]{1,0:T(8,128)}, f32[1,128]{1,0:T(1,128)}, f32[1,128]{1,0:T(1,128)}, f32[2,128,128]{2,1,0:T(8,128)}) custom-call(f32[512,256]{1,0:T(8,128)} %get-tuple-element.13.gw_in, f32[8,128]{1,0:T(8,128)} %get-tuple-element.14.small, f32[2,128,128]{2,1,0:T(8,128)} %get-tuple-element.15.vg_in), custom_call_target="tpu_custom_call" | custom-call | tf_op jit(solution)/shard_map/write_results/pallas_call | solution.py:678

commit v3 on v2

--- a/solution.py
+++ b/solution.py
@@ -37,7 +37,7 @@
 
 class Net:
     def __init__(self, send, recv):
-        self.send, self.recv, self.used, self.open = send, recv, 0, []
+        self.send, self.recv, self.n_send, self.n_recv, self.open = send, recv, 0, 0, []
         self.z = lax.axis_index("batch")
         self.c = lax.axis_index("col")
         self.core = lax.rem(self.c, 2)
@@ -57,32 +57,37 @@
     def partner(self):
         return (self.z, self.chip * 2 + 1 - self.core)
 
-    def copy(self, src, dst, device, i):
+    def copy(self, src, dst, device, send, recv):
         return pltpu.make_async_remote_copy(
             src_ref=src,
             dst_ref=dst,
-            send_sem=self.send.at[i],
-            recv_sem=self.recv.at[i],
+            send_sem=self.send.at[send],
+            recv_sem=self.recv.at[recv],
             device_id=device,
             device_id_type=MESH,
         )
 
-    def group(self, meter):
-        i = self.used
-        self.used += 1
-        whole = self.copy(meter, meter, self.partner(), i)
-        self.open.append(whole)
-        return i, whole
-
-    def push(self, src, dst, device, group=None):
+    def sends(self, meter):
+        i = self.n_send
+        self.n_send += 1
+        self.open.append(self.copy(meter, meter, self.partner(), i, 0))
+        return i
+
+    def group(self, meter, sends=None):
+        send = self.sends(meter) if sends is None else sends
+        i = self.n_recv
+        self.n_recv += 1
+        return send, i, self.copy(meter, meter, self.partner(), send, i)
+
+    def push(self, src, dst, device, group=None, sends=None):
         if group is not None:
-            self.copy(src, dst, device, group[0]).start()
+            self.copy(src, dst, device, group[0], group[1]).start()
             return None
-        i = self.used
-        self.used += 1
-        one = self.copy(src, dst, device, i)
+        send = self.sends(src) if sends is None else sends
+        i = self.n_recv
+        self.n_recv += 1
+        one = self.copy(src, dst, device, send, i)
         one.start()
-        self.open.append(one)
         return one
 
     def peers(self):
@@ -108,7 +113,7 @@
     for d in (4, 3, 5, 2, 6, 1, 7):
         net.push(buf.at[net.z], buf.at[net.z], net.at_z(d), group)
     yield
-    group[1].wait_recv()
+    group[2].wait_recv()
     yield
 
 
@@ -116,37 +121,38 @@
     group = net.group(dst)
     for k, (dy, dx) in enumerate(OFFSETS):
         net.push(src, dst.at[k], net.at(mod4(net.y + dy), mod4(net.x + dx)), group)
-    return group[1]
+    return group[2]
 
 
 def ring_z(net, buf):
+    sends = net.sends(buf.at[0:7])
     up, down = {}, {}
     for q in range(4):
         own = buf.at[net.z, q]
-        up[1, q] = net.push(own, own, net.at_z(1))
-        down[1, q] = net.push(own, own, net.at_z(7))
+        up[1, q] = net.push(own, own, net.at_z(1), sends=sends)
+        down[1, q] = net.push(own, own, net.at_z(7), sends=sends)
     yield
     for d in range(1, 5):
-        for q in range(4):
-            if d < 4 or q < 2:
-                up[d, q].wait_recv()
-                if d < 3 or (d == 3 and q < 2):
-                    block = buf.at[mod8(net.z + 8 - d), q]
-                    up[d + 1, q] = net.push(block, block, net.at_z(1))
-            if d < 4 or q >= 2:
-                down[d, q].wait_recv()
-                if d < 3 or (d == 3 and q >= 2):
-                    block = buf.at[mod8(net.z + d), q]
-                    down[d + 1, q] = net.push(block, block, net.at_z(7))
-            if q == 1 and d < 4:
-                yield
-        yield
+        for q in range(4 if d < 4 else 2):
+            up[d, q].wait_recv()
+            if d < 3 or (d == 3 and q < 2):
+                block = buf.at[mod8(net.z + 8 - d), q]
+                up[d + 1, q] = net.push(block, block, net.at_z(1), sends=sends)
+            q = q if d < 4 else q + 2
+            down[d, q].wait_recv()
+            if d < 3 or (d == 3 and q >= 2):
+                block = buf.at[mod8(net.z + d), q]
+                down[d + 1, q] = net.push(block, block, net.at_z(7), sends=sends)
+            yield
 
 
 def gather_plane(net, buf):
     first_at, then_at = (net.x, net.y), (net.y, net.x)
     shift = (0, 3, 1, 2)
     first, cross, over = {}, {}, {}
+    first_sends = net.sends(buf.at[0:3, 0, 0])
+    cross_sends = net.sends(buf.at[0:3, :, 0])
+    over_sends = net.sends(buf.at[:, :, 0])
 
     def piece(h, f, t):
         y, x = (t, f) if h == 0 else (f, t)
@@ -154,22 +160,23 @@
 
     def spread(h, j):
         f = mod4(first_at[h] + shift[j])
-        cross[h, j] = net.group(buf.at[0:3, 0, 0, 0])
+        cross[h, j] = net.group(buf.at[0:3, 0, 0, 0], cross_sends)
         block = piece(h, f, then_at[h])
         for d in (2, 1, 3):
             net.push(block, block, net.along(h, f_own[h], mod4(then_at[h] + d)), cross[h, j])
 
     def hand_over(h, j):
-        cross[h, j][1].wait_recv()
+        cross[h, j][2].wait_recv()
         f = mod4(first_at[h] + shift[j])
         line = buf.at[:, f, net.core, 0] if h == 0 else buf.at[f, :, net.core, 1]
-        over[h, j] = net.push(line, line, net.partner())
+        over[h, j] = net.push(line, line, net.partner(), sends=over_sends)
 
     f_own = first_at
     for h in range(2):
         block = piece(h, first_at[h], then_at[h])
         for d in (1, 3, 2):
-            first[h, d] = net.push(block, block, net.along(h, mod4(first_at[h] + d), then_at[h]))
+            to = net.along(h, mod4(first_at[h] + d), then_at[h])
+            first[h, d] = net.push(block, block, to, sends=first_sends)
     for h in range(2):
         spread(h, 0)
     yield
@@ -216,13 +223,17 @@
 
 
 def body(
+    views_hbm,
+    gain_hbm,
+    bias_hbm,
+    w_hbm,
+    gw_hbm,
+    small,
+    views_gradient,
     views,
     gain,
     bias,
-    w_hbm,
     grad_weight,
-    small,
-    views_gradient,
     w,
     act,
     act_t,
@@ -263,12 +274,19 @@
 ):
     net = Net(send_sems, recv_sems)
     z, y, x, core, chip = net.z, net.y, net.x, net.core, net.chip
-    load = pltpu.make_async_copy(w_hbm, w, load_sem)
-    load.start()
+    load_views = pltpu.make_async_copy(views_hbm, views, load_sem.at[0])
+    load_gain = pltpu.make_async_copy(gain_hbm, gain, load_sem.at[1])
+    load_bias = pltpu.make_async_copy(bias_hbm, bias, load_sem.at[2])
+    load = pltpu.make_async_copy(w_hbm, w, load_sem.at[3])
+    load_views.start()
     barrier = pltpu.get_barrier_semaphore()
     peers = net.peers()
     for peer in peers:
         pl.semaphore_signal(barrier, inc=1, device_id=peer, device_id_type=MESH)
+    load_gain.start()
+    load_bias.start()
+    load.start()
+    load_views.wait()
     local = []
     for v in range(2):
         t = views[v].astype(F32)
@@ -279,6 +297,8 @@
 
     g = share_z(net, stats)
     next(g)
+    load_gain.wait()
+    load_bias.wait()
     next(g)
     inverse = []
     for v in range(2):
@@ -335,15 +355,16 @@
     zb = zacc[...].astype(BF16)
     zbuf[z] = zb.reshape(4, 64, 256)
     zf = zb.astype(F32)
-    zsum[z] = rows_of([col_sum(zf[0]), col_sum(zf[1])], 256)
+    zsums = [col_sum(zf[v])[:, k : k + 128] for v in range(2) for k in (0, 128)]
+    zsum[z] = jnp.concatenate(zsums, axis=0)
     means = share_z(net, zsum)
     next(means)
+    own_rows = act_t.at[y, x, core, :, lax.div(z, 4), lax.rem(z, 4)]
+    features = net.group(kgat.at[0, 0, 0:14])
+    for d in (4, 3, 5, 2, 6, 1, 7):
+        net.push(feature_rows(mod8(z + d)), own_rows, net.at_z(d), features)
     zring = ring_z(net, zbuf)
     next(zring)
-    own_rows = act_t.at[y, x, core, :, lax.div(z, 4), lax.rem(z, 4)]
-    features = [
-        net.push(feature_rows(mod8(z + d)), own_rows, net.at_z(d)) for d in range(1, PLANES)
-    ]
     own_rows[...] = feature_rows(z)[...]
     colstat[...] = jnp.zeros_like(colstat)
 
@@ -356,22 +377,26 @@
         colstat[v : v + 1, :] += col_sum(zc * zc)
         colstat[2 + v : 3 + v, :] += col_sum(cf * cf)
         colstat[4 + v : 5 + v, :] += col_sum(cf)
-        colstat[6 + v : 7 + v, :] += col_sum(zc)
         kpart[stage, owner, 8 * v : 8 * v + 8] = dot_nt(zcb[z, v], cb).reshape(8, 16, 128)
 
     k_over, k_in, k_gat, k_done = {}, {}, {}, {}
+    k_sends = [
+        net.sends(m) for m in (kpart.at[:, 0], kin, kgat.at[:, 0, 0:15], kgat.at[:, 0])
+    ]
 
     def k_give(stage):
-        k_over[stage] = net.push(kpart.at[stage, 1 - core], krecv.at[stage], net.partner())
+        k_over[stage] = net.push(
+            kpart.at[stage, 1 - core], krecv.at[stage], net.partner(), sends=k_sends[0]
+        )
 
     def k_spread(stage):
         k_over[stage].wait_recv()
         kmine[stage] = kpart[stage, core] + krecv[stage]
-        group = net.group(kin.at[stage])
+        group = net.group(kin.at[stage], k_sends[1])
         for k, (dy, dx) in enumerate(OFFSETS):
             ty, tx = mod4(y + dy), mod4(x + dx)
             net.push(kmine.at[stage, ty * SIDE + tx], kin.at[stage, k], net.at(ty, tx), group)
-        k_in[stage] = group[1]
+        k_in[stage] = group[2]
 
     def k_gather(stage):
         k_in[stage].wait_recv()
@@ -379,14 +404,16 @@
         kown[stage] = total
         kgat[stage, core, chip] = total.astype(BF16)
         own = kgat.at[stage, core, chip]
-        group = net.group(kgat.at[stage, core, 0:15])
+        group = net.group(kgat.at[stage, core, 0:15], k_sends[2])
         for dy, dx in OFFSETS:
             net.push(own, own, net.at(mod4(y + dy), mod4(x + dx)), group)
-        k_gat[stage] = group[1]
+        k_gat[stage] = group[2]
 
     def k_hand(stage):
         k_gat[stage].wait_recv()
-        k_done[stage] = net.push(kgat.at[stage, core], kgat.at[stage, core], net.partner())
+        k_done[stage] = net.push(
+            kgat.at[stage, core], kgat.at[stage, core], net.partner(), sends=k_sends[3]
+        )
 
     def k_moved(stage):
         k_done[stage].wait_recv()
@@ -402,41 +429,48 @@
             else:
                 moved[v] = moved[v] + term
 
-    next(zring)
-    for copy in features:
-        copy.wait_recv()
+    def step(count):
+        for _ in range(count):
+            next(zring)
+
+    def blocks(stage):
+        for v in range(2):
+            block_in(stage, 0, v)
+            block_in(stage, 1, v)
+
+    step(6)
+    next(means)
+    ztotal = [
+        jnp.concatenate([col_sum(zsum[:, 2 * v + k, :]) for k in range(2)], axis=1) for v in range(2)
+    ]
+    zmean = [t / ROWS for t in ztotal]
+    block_in(3, 0, 0)
+    block_in(3, 0, 1)
+    blocks(0)
+    k_give(0)
+    features[2].wait_recv()
     agt = gather_plane(net, act_t)
     next(agt)
-    next(zring)
-    next(means)
-    zmean = [col_sum(zsum[:, v, :]) / ROWS for v in range(2)]
-    for v in range(2):
-        block_in(3, 0, v)
-    for v in range(2):
-        block_in(0, 0, v)
-        block_in(0, 1, v)
-    k_give(0)
-    next(zring)
+    step(2)
+    blocks(1)
+    k_give(1)
     k_spread(0)
-    next(agt)
-    next(zring)
-    for v in range(2):
-        block_in(1, 0, v)
-        block_in(1, 1, v)
-    k_give(1)
-    next(zring)
+    step(1)
+    next(agt)
+    step(2)
+    k_spread(1)
+    step(1)
+    blocks(2)
+    k_give(2)
+    step(1)
     k_gather(0)
-    k_spread(1)
-    next(zring)
-    for v in range(2):
-        block_in(2, 0, v)
-        block_in(2, 1, v)
-    k_give(2)
-    next(zring)
-    for v in range(2):
-        block_in(3, 1, v)
+    step(1)
+    block_in(3, 1, 0)
+    block_in(3, 1, 1)
     k_give(3)
     k_spread(2)
+    k_gather(1)
+    k_spread(3)
 
     total_rows = [split3(colstat[4 + v : 5 + v, :]) for v in range(2)]
     for v in range(2):
@@ -445,16 +479,14 @@
                 dot_nt(total_rows[v], zcb[slot, v])
             )
     r_over = net.push(rsum, rcore, net.partner())
-    k_spread(3)
-    k_gather(1)
+    k_gather(2)
+    k_hand(0)
     r_over.wait_recv()
     rmine[...] = rsum[...] + rcore[...]
     r_in = share_plane(net, rmine, rin)
-    k_gather(2)
-    k_hand(0)
+    k_hand(1)
     next(agt)
     k_gather(3)
-    k_hand(1)
     k_moved(0)
     k_hand(2)
     k_moved(1)
@@ -480,7 +512,7 @@
         mean_t.append(
             (
                 coef * (col_sum(m) - diag[v] * colstat[4 + v : 5 + v, :])
-                - hinge * colstat[6 + v : 7 + v, :]
+                - hinge * (ztotal[v] - ROWS * zmean[v])
             )
             / ROWS
         )
@@ -499,6 +531,7 @@
     first_at, then_at = (x, y), (y, x)
     dzl = [dz[z, 2 * v : 2 * v + 2].reshape(128, 256) for v in range(2)]
     d_over, d_in, d_mid = {}, {}, {}
+    d_sends = [net.sends(dgive), net.sends(dpart.at[:, 1:4])]
 
     def d_terms(h, g, parity, store):
         f = mod4(first_at[h] + g)
@@ -513,13 +546,16 @@
             return
         dpart[h, g] = (dkeep[h, g] + drecv[h, g]).astype(BF16)
         f = mod4(first_at[h] + g)
-        d_in[h, g] = net.push(dpart.at[h, g], din.at[h, g], net.along(h, f, then_at[h]))
+        to = net.along(h, f, then_at[h])
+        d_in[h, g] = net.push(dpart.at[h, g], din.at[h, g], to, sends=d_sends[1])
 
     last = None
     for g in (2, 1, 3, 0):
         for h in range(2):
             d_terms(h, g, 1 - core, dgive)
-            d_over[h, g] = net.push(dgive.at[h, g], drecv.at[h, g], net.partner())
+            d_over[h, g] = net.push(
+                dgive.at[h, g], drecv.at[h, g], net.partner(), sends=d_sends[0]
+            )
         for h in range(2):
             d_terms(h, g, core, dkeep)
         if last is not None:
@@ -527,8 +563,10 @@
                 d_send(h, last)
         last = g
     next(dring)
+    next(dring)
     for h in range(2):
         d_send(h, 0)
+    next(dring)
 
     inv_row = col_sum(diff * diff)
     hinge_row = jnp.maximum(1.0 - std[0], 0.0) + jnp.maximum(1.0 - std[1], 0.0)
@@ -545,6 +583,9 @@
     loss_core.wait_recv()
     lsend[1] = lsend[0] + lrecv[15]
     loss_in = share_plane(net, lsend.at[1], lrecv.at[0:15])
+    next(dring)
+    next(dring)
+    next(dring)
     for h in range(2):
         for g in range(1, 4):
             d_in[h, g].wait_recv()
@@ -555,11 +596,12 @@
         for k, d in enumerate((2, 1, 3)):
             t = mod4(then_at[h] + d)
             net.push(dmid.at[h, t], dmid_in.at[h, k], net.along(h, first_at[h], t), group)
-        d_mid[h] = group[1]
+        d_mid[h] = group[2]
     next(dring)
     next(dring)
     loss_in.wait_recv()
     plane_loss = lsend[1, 0:1, :] + jnp.sum(lrecv[0:15, 0:1, :], axis=0)
+    next(dring)
     next(dring)
     sums = []
     for h in range(2):
@@ -571,6 +613,7 @@
     fstat[z] = rows_of([sums[0][0], sums[1][0], sums[0][1], sums[1][1], plane_loss], 128)
     final = share_z(net, fstat)
     next(final)
+    next(dring)
     next(dring)
     next(agt)
 
@@ -591,6 +634,8 @@
 
     grad_weight[...] = jnp.zeros_like(grad_weight)
     lax.fori_loop(0, 8, gw_step, 0)
+    put = pltpu.make_async_copy(grad_weight, gw_hbm, load_sem.at[4])
+    put.start()
     next(final)
     total_b = [col_sum(fstat[:, v, :]) for v in range(2)]
     total_g = [col_sum(fstat[:, 2 + v, :]) for v in range(2)]
@@ -599,11 +644,13 @@
         views_gradient[v] = (gain[...] * inverse[v]) * (
             dpre[v] - total_b[v] / ROWS - xhat[v] * (total_g[v] / ROWS)
         )
+    put.wait()
     for copy in net.open:
         copy.wait_send()
 
 
-MESSAGES = 150
+SENDS = 24
+RECEIVES = 140
 
 
 def finish(gw_in, small, vg_in, loss, grad_weight, grad_gain, grad_bias, views_gradient):
@@ -617,6 +664,10 @@
 def shards(views, norm_scale_gain, norm_shift_bias, weight):
     vmem = pltpu.VMEM
     scratch = [
+        vmem((2, 128, 128), BF16),
+        vmem((1, 128), F32),
+        vmem((1, 128), F32),
+        vmem((512, 256), F32),
         vmem((4, 4, 2, 128, 256), BF16),
         vmem((4, 4, 2, 2, 2, 4, 16, 128), BF16),
         vmem((4, 4, 2, 2, 2, 4, 16, 128), BF16),
@@ -625,7 +676,7 @@
         vmem((8, 8, 128), F32),
         vmem((2, 128, 256), F32),
         vmem((8, 4, 64, 256), BF16),
-        vmem((8, 8, 256), F32),
+        vmem((8, 4, 128), F32),
         vmem((8, 2, 128, 256), BF16),
         vmem((8, 256), F32),
         vmem((4, 2, 16, 16, 128), F32),
@@ -651,9 +702,9 @@
         vmem((2, 8, 128), F32),
         vmem((16, 8, 128), F32),
         vmem((8, 8, 128), F32),
-        pltpu.SemaphoreType.DMA((MESSAGES,)),
-        pltpu.SemaphoreType.DMA((MESSAGES,)),
-        pltpu.SemaphoreType.DMA,
+        pltpu.SemaphoreType.DMA((SENDS,)),
+        pltpu.SemaphoreType.DMA((RECEIVES,)),
+        pltpu.SemaphoreType.DMA((5,)),
     ]
     whole = pl.BlockSpec(memory_space=pltpu.VMEM)
     made = (
@@ -664,8 +715,8 @@
     results = pl.pallas_call(
         body,
         out_shape=made,
-        in_specs=[whole, whole, whole, pl.BlockSpec(memory_space=pl.ANY)],
-        out_specs=(whole, whole, whole),
+        in_specs=[pl.BlockSpec(memory_space=pl.ANY)] * 4,
+        out_specs=(pl.BlockSpec(memory_space=pl.ANY), whole, whole),
         scratch_shapes=scratch,
         compiler_params=pltpu.CompilerParams(collective_id=0, has_side_effects=True),
         name="vicreg_step",

time: 87.3 us -> 85.9 us (0.984)
  Pallas kernels: 85.9 us -> 84.2 us
    pallas_call x1, Pallas kernels: 83.9 us -> 82.2 us  [shards(): pl.pallas_call(body, out_shape=made, in_specs=[pl.BlockSpec(memory_space=...]
where the time goes in v3:
time: 85.9 us; the launch traced here: 84.8 us
  Pallas kernels  84.2 us (98%)
    pallas_call x1, Pallas kernels, shards(): pl.pallas_call(body, out_shape=made, in_specs=[pl.BlockSpec(memory_space=...  82.2 us
    pallas_call x1, Pallas kernels, shards(): pl.pallas_call(finish, out_shape=(jax.ShapeDtypeStruct((1, 1), F32), made...  1.94 us

profile of v3, /device:TPU:8, one launch (start us, length us, event | category | flops | bytes accessed | tf_op | source)
XLA Modules:
  0.0 84.8 jit_solution(16111910817954010465)
XLA Ops:
  0.6 82.2 %vicreg_step.1 = (f32[512,256]{1,0:T(8,128)}, f32[8,128]{1,0:T(8,128)}, f32[2,128,128]{2,1,0:T(8,128)}) custom-call(bf16[2,128,128]{2,1,0:T(8,128)(2,1)} %views_hbm.1, f32[1,128]{1,0:T(1,128)} %bitcast.7, f32[1,128]{1,0:T(1,128)} %bitcast.8, bf16[4,4,2,128,256]{4,3,2,1,0:T(8,128)(2,1)} %bitcast.6), custom_call_target="tpu_custom_call" | custom-call | tf_op jit(solution)/shard_map/vicreg_step/pallas_call | solution.py:715
  82.8 1.9 %write_results.1 = (f32[1,1]{1,0:T(1,128)}, f32[512,256]{1,0:T(8,128)}, f32[1,128]{1,0:T(1,128)}, f32[1,128]{1,0:T(1,128)}, f32[2,128,128]{2,1,0:T(8,128)}) custom-call(f32[512,256]{1,0:T(8,128)} %get-tuple-element.13.gw_in, f32[8,128]{1,0:T(8,128)} %get-tuple-element.14.small, f32[2,128,128]{2,1,0:T(8,128)} %get-tuple-element.15.vg_in), custom_call_target="tpu_custom_call" | custom-call | tf_op jit(solution)/shard_map/write_results/pallas_call | solution.py:729

commit v4 on v3

--- a/solution.py
+++ b/solution.py
@@ -50,6 +50,9 @@
 
     def at(self, y, x):
         return (self.z, (y * SIDE + x) * 2 + self.core)
+
+    def other(self, y, x):
+        return (self.z, (y * SIDE + x) * 2 + 1 - self.core)
 
     def along(self, h, f, t):
         return self.at(t, f) if h == 0 else self.at(f, t)
@@ -93,7 +96,9 @@
     def peers(self):
         found = [self.partner()]
         found += [self.at_z(d) for d in range(1, PLANES)]
-        found += [self.at(mod4(self.y + dy), mod4(self.x + dx)) for dy, dx in OFFSETS]
+        for dy, dx in OFFSETS:
+            found.append(self.at(mod4(self.y + dy), mod4(self.x + dx)))
+            found.append(self.other(mod4(self.y + dy), mod4(self.x + dx)))
         return found
 
 
@@ -146,7 +151,7 @@
             yield
 
 
-def gather_plane(net, buf):
+def gather_plane(net, buf, late=False):
     first_at, then_at = (net.x, net.y), (net.y, net.x)
     shift = (0, 3, 1, 2)
     first, cross, over = {}, {}, {}
@@ -185,6 +190,15 @@
             first[h, d].wait_recv()
             spread(h, j)
     yield
+    if late:
+        for j in range(4):
+            for h in range(2):
+                hand_over(h, j)
+        yield
+        for copy in over.values():
+            copy.wait_recv()
+        yield
+        return
     for j in range(4):
         for h in range(2):
             hand_over(h, j)
@@ -381,7 +395,7 @@
 
     k_over, k_in, k_gat, k_done = {}, {}, {}, {}
     k_sends = [
-        net.sends(m) for m in (kpart.at[:, 0], kin, kgat.at[:, 0, 0:15], kgat.at[:, 0])
+        net.sends(m) for m in (kpart.at[:, 0], kin, kgat.at[:, 0, 0:15], kgat.at[0:3, 0])
     ]
 
     def k_give(stage):
@@ -405,8 +419,15 @@
         kgat[stage, core, chip] = total.astype(BF16)
         own = kgat.at[stage, core, chip]
         group = net.group(kgat.at[stage, core, 0:15], k_sends[2])
+        both = net.group(kgat.at[stage, core]) if stage == 3 else None
         for dy, dx in OFFSETS:
-            net.push(own, own, net.at(mod4(y + dy), mod4(x + dx)), group)
+            ty, tx = mod4(y + dy), mod4(x + dx)
+            net.push(own, own, net.at(ty, tx), group)
+            if both is not None:
+                net.push(own, own, net.other(ty, tx), both)
+        if both is not None:
+            net.push(own, own, net.partner(), both)
+            k_done[stage] = both[2]
         k_gat[stage] = group[2]
 
     def k_hand(stage):
@@ -449,7 +470,7 @@
     blocks(0)
     k_give(0)
     features[2].wait_recv()
-    agt = gather_plane(net, act_t)
+    agt = gather_plane(net, act_t, late=True)
     next(agt)
     step(2)
     blocks(1)
@@ -464,58 +485,50 @@
     k_give(2)
     step(1)
     k_gather(0)
+    k_spread(2)
     step(1)
     block_in(3, 1, 0)
     block_in(3, 1, 1)
     k_give(3)
-    k_spread(2)
+    k_spread(3)
+
+    for v in range(2):
+        total = split3(colstat[4 + v : 5 + v, :])
+        r = col_sum(dot_nt(total, zcb[:, v].reshape(1024, 256)))
+        for slot in range(PLANES):
+            rsum[v * PLANES + slot : v * PLANES + slot + 1, :] = r[:, 128 * slot : 128 * slot + 128]
+    r_over = net.push(rsum, rcore, net.partner())
     k_gather(1)
-    k_spread(3)
-
-    total_rows = [split3(colstat[4 + v : 5 + v, :]) for v in range(2)]
-    for v in range(2):
-        for slot in range(PLANES):
-            rsum[v * PLANES + slot : v * PLANES + slot + 1, :] = col_sum(
-                dot_nt(total_rows[v], zcb[slot, v])
-            )
-    r_over = net.push(rsum, rcore, net.partner())
+    k_hand(0)
     k_gather(2)
-    k_hand(0)
     r_over.wait_recv()
     rmine[...] = rsum[...] + rcore[...]
     r_in = share_plane(net, rmine, rin)
+    k_gather(3)
     k_hand(1)
-    next(agt)
-    k_gather(3)
     k_moved(0)
     k_hand(2)
     k_moved(1)
     r_in.wait_recv()
     row_total = rmine[...] + jnp.sum(rin[...], axis=0)
-    k_hand(3)
-    k_moved(2)
-    next(agt)
-    next(agt)
-    next(agt)
-    next(agt)
-    next(agt)
-    next(agt)
     std, diag, mean_t = [], [], []
     for v in range(2):
         std.append(jnp.sqrt(colstat[v : v + 1, :] / (ROWS - 1) + eps_std))
         diag.append(colstat[2 + v : 3 + v, :])
-        m = jnp.zeros((8, 256), F32)
-        for slot in range(PLANES):
-            r = v * PLANES + slot
-            m = m + dot_nn(split3(row_total[r : r + 1, :]), zcb[slot, v])
+        row = jnp.concatenate(
+            [row_total[v * PLANES + slot : v * PLANES + slot + 1, :] for slot in range(PLANES)], axis=1
+        )
+        m = col_sum(dot_nn(split3(row), zcb[:, v].reshape(1024, 256)))
         hinge = jnp.where(std[v] < 1.0, hinge_coef, 0.0) / std[v]
         mean_t.append(
             (
-                coef * (col_sum(m) - diag[v] * colstat[4 + v : 5 + v, :])
+                coef * (m - diag[v] * colstat[4 + v : 5 + v, :])
                 - hinge * (ztotal[v] - ROWS * zmean[v])
             )
             / ROWS
         )
+    k_moved(2)
+    k_gat[3].wait_recv()
     k_moved(3)
     zl = [zbuf[z, 2 * v : 2 * v + 2].reshape(128, 256).astype(F32) for v in range(2)]
     diff = zl[0] - zl[1]
@@ -531,7 +544,7 @@
     first_at, then_at = (x, y), (y, x)
     dzl = [dz[z, 2 * v : 2 * v + 2].reshape(128, 256) for v in range(2)]
     d_over, d_in, d_mid = {}, {}, {}
-    d_sends = [net.sends(dgive), net.sends(dpart.at[:, 1:4])]
+    d_sends = [net.sends(dgive), net.sends(dpart.at[:, 1:4]), net.sends(dmid_in)]
 
     def d_terms(h, g, parity, store):
         f = mod4(first_at[h] + g)
@@ -540,15 +553,20 @@
         for k in range(4):
             store[h, g, k] = t[:, 128 * k : 128 * k + 128]
 
-    def d_send(h, g):
+    def d_ready(h, g):
         d_over[h, g].wait_recv()
-        if g == 0:
-            return
-        dpart[h, g] = (dkeep[h, g] + drecv[h, g]).astype(BF16)
-        f = mod4(first_at[h] + g)
-        to = net.along(h, f, then_at[h])
-        d_in[h, g] = net.push(dpart.at[h, g], din.at[h, g], to, sends=d_sends[1])
-
+        if g > 0:
+            dpart[h, g] = (dkeep[h, g] + drecv[h, g]).astype(BF16)
+
+    def d_send(h, g, pieces):
+        to = net.along(h, mod4(first_at[h] + g), then_at[h])
+        for k in pieces:
+            t = mod4(then_at[h] + k)
+            net.push(dpart.at[h, g, t], din.at[h, g - 1, t], to, d_in[h, k])
+
+    for h in range(2):
+        for k in range(4):
+            d_in[h, k] = net.group(din.at[h, :, 0], d_sends[1])
     last = None
     for g in (2, 1, 3, 0):
         for h in range(2):
@@ -560,13 +578,31 @@
             d_terms(h, g, core, dkeep)
         if last is not None:
             for h in range(2):
-                d_send(h, last)
+                d_ready(h, last)
+                d_send(h, last, (2, 1))
         last = g
-    next(dring)
-    next(dring)
-    for h in range(2):
-        d_send(h, 0)
-    next(dring)
+    for g in (2, 1, 3):
+        for h in range(2):
+            d_send(h, g, (3, 0))
+    next(dring)
+    next(dring)
+    for h in range(2):
+        d_ready(h, 0)
+    next(dring)
+
+    def d_sum(h, k):
+        t = mod4(then_at[h] + k)
+        d_in[h, k][2].wait_recv()
+        dmid[h, t] = (dkeep[h, 0, t] + drecv[h, 0, t]) + (
+            din[h, 0, t].astype(F32) + din[h, 1, t].astype(F32) + din[h, 2, t].astype(F32)
+        )
+        if k > 0:
+            net.push(
+                dmid.at[h, t], dmid_in.at[h, k - 1], net.along(h, first_at[h], t), d_mid[h]
+            )
+
+    for h in range(2):
+        d_mid[h] = net.group(dmid_in.at[h], d_sends[2])
 
     inv_row = col_sum(diff * diff)
     hinge_row = jnp.maximum(1.0 - std[0], 0.0) + jnp.maximum(1.0 - std[1], 0.0)
@@ -579,33 +615,31 @@
     lsend[0] = rows_of([share], 128)
     loss_core = net.push(lsend.at[0], lrecv.at[15], net.partner())
     next(dring)
+    for h in range(2):
+        d_sum(h, 2)
+    next(dring)
+    for h in range(2):
+        d_sum(h, 1)
     next(dring)
     loss_core.wait_recv()
     lsend[1] = lsend[0] + lrecv[15]
     loss_in = share_plane(net, lsend.at[1], lrecv.at[0:15])
     next(dring)
-    next(dring)
-    next(dring)
-    for h in range(2):
-        for g in range(1, 4):
-            d_in[h, g].wait_recv()
-        dmid[h] = dkeep[h, 0] + drecv[h, 0] + (
-            din[h, 1].astype(F32) + din[h, 2].astype(F32) + din[h, 3].astype(F32)
-        )
-        group = net.group(dmid_in.at[h])
-        for k, d in enumerate((2, 1, 3)):
-            t = mod4(then_at[h] + d)
-            net.push(dmid.at[h, t], dmid_in.at[h, k], net.along(h, first_at[h], t), group)
-        d_mid[h] = group[2]
-    next(dring)
-    next(dring)
+    for h in range(2):
+        d_sum(h, 3)
+    next(dring)
+    for h in range(2):
+        d_sum(h, 0)
+    next(dring)
+    next(dring)
+    next(agt)
     loss_in.wait_recv()
     plane_loss = lsend[1, 0:1, :] + jnp.sum(lrecv[0:15, 0:1, :], axis=0)
     next(dring)
     next(dring)
     sums = []
     for h in range(2):
-        d_mid[h].wait_recv()
+        d_mid[h][2].wait_recv()
         d_act = dmid[h, then_at[h]] + dmid_in[h, 0] + dmid_in[h, 1] + dmid_in[h, 2]
         dp = d_act * slope[h]
         dpre[h] = dp
@@ -650,7 +684,7 @@
 
 
 SENDS = 24
-RECEIVES = 140
+RECEIVES = 142
 
 
 def finish(gw_in, small, vg_in, loss, grad_weight, grad_gain, grad_bias, views_gradient):
@@ -695,7 +729,7 @@
         vmem((2, 4, 4, 128, 128), F32),
         vmem((2, 4, 4, 128, 128), F32),
         vmem((2, 4, 4, 128, 128), BF16),
-        vmem((2, 4, 4, 128, 128), BF16),
+        vmem((2, 3, 4, 128, 128), BF16),
         vmem((2, 4, 128, 128), F32),
         vmem((2, 3, 128, 128), F32),
         vmem((2, 128, 128), F32),

time: 85.9 us -> 82.3 us (0.958); the launches traced: 84.8 us -> 82.2 us
  Pallas kernels: 84.2 us -> 81.6 us
    pallas_call x1, Pallas kernels: 82.2 us -> 79.6 us  [shards(): pl.pallas_call(body, out_shape=made, in_specs=[pl.BlockSpec(memory_space=...]
where the time goes in v4:
time: 82.3 us; the launch traced here: 82.2 us
  Pallas kernels  81.6 us (99%)
    pallas_call x1, Pallas kernels, shards(): pl.pallas_call(body, out_shape=made, in_specs=[pl.BlockSpec(memory_space=...  79.6 us
    pallas_call x1, Pallas kernels, shards(): pl.pallas_call(finish, out_shape=(jax.ShapeDtypeStruct((1, 1), F32), made...  1.94 us

profile of v4, /device:TPU:8, one launch (start us, length us, event | category | flops | bytes accessed | tf_op | source)
XLA Modules:
  0.0 82.2 jit_solution(16072480548516656666)
XLA Ops:
  0.6 79.6 %vicreg_step.1 = (f32[512,256]{1,0:T(8,128)}, f32[8,128]{1,0:T(8,128)}, f32[2,128,128]{2,1,0:T(8,128)}) custom-call(bf16[2,128,128]{2,1,0:T(8,128)(2,1)} %views_hbm.1, f32[1,128]{1,0:T(1,128)} %bitcast.7, f32[1,128]{1,0:T(1,128)} %bitcast.8, bf16[4,4,2,128,256]{4,3,2,1,0:T(8,128)(2,1)} %bitcast.6), custom_call_target="tpu_custom_call" | custom-call | tf_op jit(solution)/shard_map/vicreg_step/pallas_call | solution.py:749
  80.3 1.9 %write_results.1 = (f32[1,1]{1,0:T(1,128)}, f32[512,256]{1,0:T(8,128)}, f32[1,128]{1,0:T(1,128)}, f32[1,128]{1,0:T(1,128)}, f32[2,128,128]{2,1,0:T(8,128)}) custom-call(f32[512,256]{1,0:T(8,128)} %get-tuple-element.13.gw_in, f32[8,128]{1,0:T(8,128)} %get-tuple-element.14.small, f32[2,128,128]{2,1,0:T(8,128)} %get-tuple-element.15.vg_in), custom_call_target="tpu_custom_call" | custom-call | tf_op jit(solution)/shard_map/write_results/pallas_call | solution.py:763

commit v5 on v4

--- a/solution.py
+++ b/solution.py
@@ -182,9 +182,12 @@
         for d in (1, 3, 2):
             to = net.along(h, mod4(first_at[h] + d), then_at[h])
             first[h, d] = net.push(block, block, to, sends=first_sends)
+    if late:
+        yield
     for h in range(2):
         spread(h, 0)
-    yield
+    if not late:
+        yield
     for j, d in ((1, 1), (2, 3), (3, 2)):
         for h in range(2):
             first[h, d].wait_recv()
@@ -374,11 +377,11 @@
     means = share_z(net, zsum)
     next(means)
     own_rows = act_t.at[y, x, core, :, lax.div(z, 4), lax.rem(z, 4)]
+    zring = ring_z(net, zbuf)
+    next(zring)
     features = net.group(kgat.at[0, 0, 0:14])
     for d in (4, 3, 5, 2, 6, 1, 7):
         net.push(feature_rows(mod8(z + d)), own_rows, net.at_z(d), features)
-    zring = ring_z(net, zbuf)
-    next(zring)
     own_rows[...] = feature_rows(z)[...]
     colstat[...] = jnp.zeros_like(colstat)
 
@@ -469,14 +472,13 @@
     block_in(3, 0, 1)
     blocks(0)
     k_give(0)
-    features[2].wait_recv()
-    agt = gather_plane(net, act_t, late=True)
-    next(agt)
     step(2)
     blocks(1)
     k_give(1)
     k_spread(0)
     step(1)
+    features[2].wait_recv()
+    agt = gather_plane(net, act_t, late=True)
     next(agt)
     step(2)
     k_spread(1)
@@ -505,6 +507,7 @@
     rmine[...] = rsum[...] + rcore[...]
     r_in = share_plane(net, rmine, rin)
     k_gather(3)
+    next(agt)
     k_hand(1)
     k_moved(0)
     k_hand(2)

time: 82.3 us -> 78.9 us (0.959)
  Pallas kernels: 81.6 us -> 77.7 us
    pallas_call x1, Pallas kernels: 79.6 us -> 75.7 us  [shards(): pl.pallas_call(body, out_shape=made, in_specs=[pl.BlockSpec(memory_space=...]
where the time goes in v5:
time: 78.9 us; the launch traced here: 78.3 us
  Pallas kernels  77.7 us (98%)
    pallas_call x1, Pallas kernels, shards(): pl.pallas_call(body, out_shape=made, in_specs=[pl.BlockSpec(memory_space=...  75.7 us
    pallas_call x1, Pallas kernels, shards(): pl.pallas_call(finish, out_shape=(jax.ShapeDtypeStruct((1, 1), F32), made...  1.94 us

profile of v5, /device:TPU:8, one launch (start us, length us, event | category | flops | bytes accessed | tf_op | source)
XLA Modules:
  0.0 78.3 jit_solution(5516050805542332609)
XLA Ops:
  0.6 75.7 %vicreg_step.1 = (f32[512,256]{1,0:T(8,128)}, f32[8,128]{1,0:T(8,128)}, f32[2,128,128]{2,1,0:T(8,128)}) custom-call(bf16[2,128,128]{2,1,0:T(8,128)(2,1)} %views_hbm.1, f32[1,128]{1,0:T(1,128)} %bitcast.7, f32[1,128]{1,0:T(1,128)} %bitcast.8, bf16[4,4,2,128,256]{4,3,2,1,0:T(8,128)(2,1)} %bitcast.6), custom_call_target="tpu_custom_call" | custom-call | tf_op jit(solution)/shard_map/vicreg_step/pallas_call | solution.py:752
  76.4 1.9 %write_results.1 = (f32[1,1]{1,0:T(1,128)}, f32[512,256]{1,0:T(8,128)}, f32[1,128]{1,0:T(1,128)}, f32[1,128]{1,0:T(1,128)}, f32[2,128,128]{2,1,0:T(8,128)}) custom-call(f32[512,256]{1,0:T(8,128)} %get-tuple-element.13.gw_in, f32[8,128]{1,0:T(8,128)} %get-tuple-element.14.small, f32[2,128,128]{2,1,0:T(8,128)} %get-tuple-element.15.vg_in), custom_call_target="tpu_custom_call" | custom-call | tf_op jit(solution)/shard_map/write_results/pallas_call | solution.py:766

commit v6 on v5

--- a/solution.py
+++ b/solution.py
@@ -583,6 +583,8 @@
             for h in range(2):
                 d_ready(h, last)
                 d_send(h, last, (2, 1))
+        if g == 3:
+            next(dring)
         last = g
     for g in (2, 1, 3):
         for h in range(2):
@@ -639,7 +641,6 @@
     loss_in.wait_recv()
     plane_loss = lsend[1, 0:1, :] + jnp.sum(lrecv[0:15, 0:1, :], axis=0)
     next(dring)
-    next(dring)
     sums = []
     for h in range(2):
         d_mid[h][2].wait_recv()
@@ -656,8 +657,8 @@
 
     def gw_step(i, carry):
         lhs, rhs = [], []
-        for k in range(2):
-            c = 2 * i + k
+        for k in range(4):
+            c = 4 * i + k
             cy, cx = lax.div(c, 4), lax.rem(c, 4)
             lhs.append(
                 jnp.concatenate(
@@ -670,7 +671,7 @@
         return carry
 
     grad_weight[...] = jnp.zeros_like(grad_weight)
-    lax.fori_loop(0, 8, gw_step, 0)
+    lax.fori_loop(0, 4, gw_step, 0)
     put = pltpu.make_async_copy(grad_weight, gw_hbm, load_sem.at[4])
     put.start()
     next(final)

time: 78.9 us -> 78.5 us (level)
  no operation moved by 1% of the time
where the time goes in v6:
time: 78.5 us; the launch traced here: 78.4 us
  Pallas kernels  77.8 us (99%)
    pallas_call x1, Pallas kernels, shards(): pl.pallas_call(body, out_shape=made, in_specs=[pl.BlockSpec(memory_space=...  75.8 us
    pallas_call x1, Pallas kernels, shards(): pl.pallas_call(finish, out_shape=(jax.ShapeDtypeStruct((1, 1), F32), made...  1.94 us

profile of v6, /device:TPU:8, one launch (start us, length us, event | category | flops | bytes accessed | tf_op | source)
XLA Modules:
  0.0 78.4 jit_solution(3580617320588696644)
XLA Ops:
  0.6 75.8 %vicreg_step.1 = (f32[512,256]{1,0:T(8,128)}, f32[8,128]{1,0:T(8,128)}, f32[2,128,128]{2,1,0:T(8,128)}) custom-call(bf16[2,128,128]{2,1,0:T(8,128)(2,1)} %views_hbm.1, f32[1,128]{1,0:T(1,128)} %bitcast.7, f32[1,128]{1,0:T(1,128)} %bitcast.8, bf16[4,4,2,128,256]{4,3,2,1,0:T(8,128)(2,1)} %bitcast.6), custom_call_target="tpu_custom_call" | custom-call | tf_op jit(solution)/shard_map/vicreg_step/pallas_call | solution.py:753
  76.4 1.9 %write_results.1 = (f32[1,1]{1,0:T(1,128)}, f32[512,256]{1,0:T(8,128)}, f32[1,128]{1,0:T(1,128)}, f32[1,128]{1,0:T(1,128)}, f32[2,128,128]{2,1,0:T(8,128)}) custom-call(f32[512,256]{1,0:T(8,128)} %get-tuple-element.13.gw_in, f32[8,128]{1,0:T(8,128)} %get-tuple-element.14.small, f32[2,128,128]{2,1,0:T(8,128)} %get-tuple-element.15.vg_in), custom_call_target="tpu_custom_call" | custom-call | tf_op jit(solution)/shard_map/write_results/pallas_call | solution.py:767
